TPU v7x, 256 devices: a whole 4x4x8 slice. The times are simulated.
256 devices in a mesh: chain: 64 (over z, x, core), term: 4 (over y).
Axes of the slice: x: 4, y: 4, z: 8, core: 2. Of those that a mesh axis runs over, the one named last changes fastest.
Arguments:
- psi_guess: float32 [64, 8, 128, 128], P('chain'), may hold values from -6 to 6
- transfer_raw: float32 [64, 8, 128, 128], P('chain'), may hold values from -6 to 6
- left_env: float32 [64, 32, 8, 128, 128], P('chain', 'term'), may hold values from -0.75 to 0.75
- right_env: float32 [64, 32, 8, 128, 128], P('chain', 'term'), may hold values from -0.75 to 0.75
- block_sizes: int32 [64, 2, 8], P('chain'), may hold values from 64 to 128
Outputs:
- psi_out: float32 [64, 8, 128, 128], P('chain', 'term')
- energy: float32 [64], P('chain')
All inputs are finite; a program needn't handle non-finite values.
Results may differ from a plain program's by a relative error of at most 0.0003.
Values sent between devices are 32-bit elements; how exact they have to be, the bound alone decides.
No kernel may reach another device: no remote copies, remote signals or barrier semaphores. Data moves between devices by JAX's collectives and lax.ppermute only.
A program may use at most 128 MiB of HBM per device.

v0:
```python
import math

import jax
import jax.numpy as jnp
from jax import lax
from jax.sharding import PartitionSpec as P

ITERS = 4


precise = lax.Precision.HIGHEST
twist_scale = 0.22
shrink = 1.047
epsilon = 1e-06


def from_behind(value, axis, steps):
    count = lax.axis_size(axis)
    leading, last = (max(0, -steps), min(count, count - steps))
    return lax.ppermute(value, axis, [(source, source + steps) for source in range(leading, last)])


def transfer(raw_normal):
    block_len = raw_normal.shape[-1]
    identity = jnp.eye(block_len, dtype=jnp.float32)
    skewed = (raw_normal - jnp.swapaxes(raw_normal, -1, -2)) * (
        twist_scale / math.sqrt(2.0 * block_len)
    )
    return (identity + skewed) / shrink


def symmetric(raw_normal):
    return 0.5 * (raw_normal + jnp.swapaxes(raw_normal, -1, -2))


def sector_mask(sizes_pair, block_len):
    positions = jnp.arange(block_len, dtype=jnp.int32)
    row_live = (positions[None, :] < sizes_pair[0][:, None]).astype(jnp.float32)
    col_live = (positions[None, :] < sizes_pair[1][:, None]).astype(jnp.float32)
    return row_live[:, :, None] * col_live[:, None, :]


def local(psi_guess, transfer_raw, left_env, right_env, block_sizes):
    blocks = transfer(transfer_raw[0])
    sectors = blocks.shape[0]
    block_len = blocks.shape[-1]
    identity = jnp.broadcast_to(jnp.eye(block_len, dtype=jnp.float32), blocks.shape)
    position = lax.axis_index("chain")
    segments = lax.axis_size("chain")
    from_left, left_blocks = from_behind((left_env[0], blocks), "chain", 1)
    from_right, right_blocks = from_behind((right_env[0], blocks), "chain", -1)
    is_first = position == 0
    is_last = position == segments - 1
    prefix = jnp.where(is_first, identity, left_blocks)
    suffix = jnp.where(is_last, identity, right_blocks)
    left_sym = symmetric(jnp.where(is_first, left_env[0], from_left))
    right_sym = symmetric(jnp.where(is_last, right_env[0], from_right))
    live_mask = sector_mask(block_sizes[0], block_len)
    groups = lax.axis_size("term")
    owned = sectors // groups
    offset = lax.axis_index("term") * owned
    volume = float(sectors * block_len * block_len)
    partway = jnp.einsum("tkjl,klm->tkjm", left_sym, prefix, precision=precise)
    left_full = jnp.einsum("kji,tkjm->tkim", prefix, partway, precision=precise)
    partway = jnp.einsum("kij,tkjl->tkil", suffix, right_sym, precision=precise)
    right_full = jnp.einsum("tkil,kml->tkim", partway, suffix, precision=precise)

    def partial_term(vector):
        halfway = jnp.einsum("tkij,kjl->tkil", left_full, vector, precision=precise)
        return jnp.einsum("tkil,tklm->kim", halfway, right_full, precision=precise)

    def finish(summed):
        return live_mask * summed

    started = live_mask * psi_guess[0]
    start_norm = jnp.sqrt(jnp.sum(started * started) / volume + epsilon)
    vector = started / start_norm

    def apply_whole(direction):
        return finish(lax.psum(partial_term(direction), "term"))

    def mean_dot(first_arr, second_arr):
        return jnp.sum(first_arr * second_arr) / volume

    image = apply_whole(vector)
    energy = mean_dot(vector, image)
    for step_index in range(ITERS):
        residual = image - energy * vector
        res_norm = jnp.sqrt(mean_dot(residual, residual) + epsilon)
        along = mean_dot(residual, image) / res_norm
        unit_dir = residual / res_norm
        image_unit = apply_whole(unit_dir)
        curve = mean_dot(unit_dir, image_unit)
        gap_half = 0.5 * (curve - energy)
        lowest = 0.5 * (curve + energy) - jnp.sqrt(gap_half * gap_half + along * along)
        coef_b = lowest - energy
        combined = jnp.sqrt(along * along + coef_b * coef_b)
        vector = (along * vector + coef_b * unit_dir) / combined
        image = (along * image + coef_b * image_unit) / combined
        energy = lowest
    vector_share = lax.dynamic_slice_in_dim(vector, offset, owned, 0)
    return (vector_share[None], jnp.reshape(energy, (1,)))


def solution(mesh):
    placed = (
        P("chain", None, None, None),
        P("chain", None, None, None),
        P("chain", "term", None, None, None),
        P("chain", "term", None, None, None),
        P("chain", None, None),
    )
    return jax.shard_map(
        local,
        mesh=mesh,
        in_specs=placed,
        out_specs=(P("chain", "term", None, None), P("chain")),
        check_vma=False,
    )
```

profile of v0, /device:TPU:2, one launch (start us, length us, event | category | flops | bytes accessed | tf_op | source)
XLA Modules:
  0.0 458.2 jit_solution(8209784709253944239)
XLA Ops:
  7.2 5.4 %copy.8 = f32[1,8,8,128,128]{3,4,2,1,0:T(8,128)} copy(f32[1,8,8,128,128]{4,3,2,1,0:T(8,128)} %param.7) | data formatting | bytes 8388608 | tf_op args[2]
  26.0 36.8 %collective-permute-done.1 = f32[8,8,128,128]{2,3,1,0:T(8,128)} collective-permute-done((f32[8,8,128,128]{2,3,1,0:T(8,128)}, f32[8,8,128,128]{2,3,1,0:T(8,128)}, u32[]{:S(2)}, u32[]{:S(2)}) %collective-permute-start.1) | collective-permute-done | bytes 4194336 | tf_op jit(solution)/shard_map/ppermute | solution.py:20
  62.8 6.5 %broadcast_select_fusion.1 = f32[8,8,128,128]{2,3,1,0:T(8,128)} fusion(f32[8,8,128,128]{2,3,1,0:T(8,128)} %collective-permute-done.1, pred[]{:T(512)S(6)} %eq.18, f32[1,8,8,128,128]{3,4,2,1,0:T(8,128)} %copy.8), kind=kLoop, calls=%fused_computation.38 | loop fusion | flops 1048576 | bytes 12582913 | tf_op jit(solution)/shard_map/jit(_where)/select_n | solution.py:56
  69.3 5.5 %copy.9 = f32[8,8,128,128]{3,2,1,0:T(8,128)} copy(f32[8,8,128,128]{2,3,1,0:T(8,128)} %broadcast_select_fusion.1) | data formatting | bytes 8388608 | tf_op jit(solution)/shard_map/jit(_where)/select_n | solution.py:56
  74.8 6.7 %broadcast_select_fusion = f32[8,8,128,128]{3,2,1,0:T(8,128)} fusion(f32[8,8,128,128]{3,2,1,0:T(8,128)} %collective-permute-done.3, pred[]{:T(512)S(6)} %eq.20, f32[1,8,8,128,128]{4,3,2,1,0:T(8,128)} %param.8), kind=kLoop, calls=%fused_computation.37 | loop fusion | flops 1048576 | bytes 12582913 | tf_op jit(solution)/shard_map/jit(_where)/select_n | solution.py:57
  85.7 5.1 %fusion.28 = f32[8,8,128,128]{3,2,1,0:T(8,128)} fusion(f32[8,128,8,128]{3,1,2,0:T(8,128)S(1)} %fusion.33, f32[8,128,128]{2,1,0:T(8,128)S(1)} %collective-permute-done, f32[128,128]{1,0:T(8,128)S(1)} %fusion.90, pred[]{:T(512)S(6)} %eq.18), kind=kOutput, calls=%fused_computation.29 | convolution fusion | flops 1610743808 | bytes 8978433 | tf_op jit(solution)/shard_map/kji,tkjm->tkim/dot_general | solution.py:64
  90.8 5.3 %copy.10 = f32[8,8,128,128]{2,3,1,0:T(8,128)} copy(f32[8,8,128,128]{3,2,1,0:T(8,128)} %broadcast_select_fusion) | data formatting | bytes 8388608 | tf_op jit(solution)/shard_map/jit(_where)/select_n | solution.py:57
  96.1 9.0 %fusion.26 = f32[8,128,8,128]{1,3,2,0:T(8,128)S(1)} fusion(f32[8,8,128,128]{3,2,1,0:T(8,128)} %fusion.28, f32[1,8,128,128]{3,2,1,0:T(8,128)S(1)} %copy-done.7, f32[]{:T(128)S(6)} %sqrt.39, f32[8,128]{1,0:T(8,128)S(1)} %get-tuple-element.21, f32[8,128]{1,0:T(8,128)S(1)} %get-tuple-element.20), kind=kOutput, calls=%fused_computation.27 | convolution fusion | flops 1611005952 | bytes 8921092 | tf_op jit(solution)/shard_map/tkij,kjl->tkil/dot_general | solution.py:69
  105.2 4.4 fusion.31
  109.6 4.3 fusion.14
  115.9 5.3 %fusion.35 = f32[8,128,128]{2,1,0:T(8,128)} fusion(f32[8,128,8,128]{3,1,2,0:T(8,128)S(1)} %fusion.14, f32[8,128,8,128]{1,3,2,0:T(8,128)S(1)} %fusion.26), kind=kOutput, calls=%fused_computation.45 | convolution fusion | flops 1610612736 | bytes 8912896 | tf_op jit(solution)/shard_map/tkil,tklm->kim/dot_general | solution.py:70
  121.2 52.0 %all-reduce.6.cloned.1.call-done = f32[8,128,128]{2,1,0:T(8,128)} async-done(((f32[8,128,128]{2,1,0:T(8,128)}), f32[8,128,128]{2,1,0:T(8,128)}) %all-reduce.6.cloned.1.call-update) | async-done | bytes 524304 | tf_op jit(solution)/shard_map/psum | solution.py:80
  178.3 8.9 %fusion.24 = f32[8,128,8,128]{1,3,2,0:T(8,128)S(1)} fusion(f32[8,8,128,128]{3,2,1,0:T(8,128)} %fusion.28, f32[]{:T(128)S(6)} %sqrt.40, f32[]{:T(128)S(6)} %div.131, f32[8,128,128]{2,1,0:T(8,128)} %all-reduce.6.cloned.1.call-done, f32[8,128]{1,0:T(8,128)S(1)} %get-tuple-element.21, f32[8,128]{1,0:T(8,128)S(1)} %get-tuple-element.20, ...), kind=kOutput, calls=%fused_computation.25 | convolution fusion | flops 1611530240 | bytes 9445388 | tf_op jit(solution)/shard_map/tkij,kjl->tkil/dot_general | solution.py:69
  187.3 4.8 %fusion.40 = f32[8,128,128]{2,1,0:T(8,128)} fusion(f32[8,128,8,128]{3,1,2,0:T(8,128)S(1)} %copy-done.1, f32[8,128,8,128]{1,3,2,0:T(8,128)S(1)} %fusion.24), kind=kOutput, calls=%fused_computation.46 | convolution fusion | flops 1610612736 | bytes 8912896 | tf_op jit(solution)/shard_map/tkil,tklm->kim/dot_general | solution.py:70
  192.1 48.8 %all-reduce.8.cloned.1.call-done = f32[8,128,128]{2,1,0:T(8,128)} async-done(((f32[8,128,128]{2,1,0:T(8,128)}), f32[8,128,128]{2,1,0:T(8,128)}) %all-reduce.8.cloned.1.call-update) | async-done | bytes 524304 | tf_op jit(solution)/shard_map/psum | solution.py:80
  247.1 8.8 %fusion.22 = f32[8,128,8,128]{1,3,2,0:T(8,128)S(1)} fusion(f32[8,8,128,128]{3,2,1,0:T(8,128)} %fusion.28, f32[]{:T(128)S(6)} %sqrt.43, f32[8,128,128]{2,1,0:T(8,128)S(1)} %get-tuple-element.17, f32[8,128,128]{2,1,0:T(8,128)S(1)} %get-tuple-element.16, f32[]{:T(128)S(6)} %sub.54), kind=kOutput, calls=%fused_computation.23 | convolution fusion | flops 1611005952 | bytes 9437192 | tf_op jit(solution)/shard_map/tkij,kjl->tkil/dot_general | solution.py:69
  255.9 4.8 %fusion.45 = f32[8,128,128]{2,1,0:T(8,128)} fusion(f32[8,128,8,128]{3,1,2,0:T(8,128)S(1)} %copy-done.2, f32[8,128,8,128]{1,3,2,0:T(8,128)S(1)} %fusion.22), kind=kOutput, calls=%fused_computation.47 | convolution fusion | flops 1610612736 | bytes 8912896 | tf_op jit(solution)/shard_map/tkil,tklm->kim/dot_general | solution.py:70
  260.8 48.8 %all-reduce.10.cloned.1.call-done = f32[8,128,128]{2,1,0:T(8,128)} async-done(((f32[8,128,128]{2,1,0:T(8,128)}), f32[8,128,128]{2,1,0:T(8,128)}) %all-reduce.10.cloned.1.call-update) | async-done | bytes 524304 | tf_op jit(solution)/shard_map/psum | solution.py:80
  315.6 8.9 %fusion.20 = f32[8,128,8,128]{1,3,2,0:T(8,128)S(1)} fusion(f32[8,8,128,128]{3,2,1,0:T(8,128)} %fusion.28, f32[]{:T(128)S(6)} %sqrt.46, f32[8,128,128]{2,1,0:T(8,128)S(1)} %get-tuple-element.14, f32[8,128,128]{2,1,0:T(8,128)S(1)} %get-tuple-element.13, f32[]{:T(128)S(6)} %sub.58), kind=kOutput, calls=%fused_computation.21 | convolution fusion | flops 1611005952 | bytes 9437192 | tf_op jit(solution)/shard_map/tkij,kjl->tkil/dot_general | solution.py:69
  324.5 4.8 %fusion.50 = f32[8,128,128]{2,1,0:T(8,128)} fusion(f32[8,128,8,128]{3,1,2,0:T(8,128)S(1)} %copy-done.3, f32[8,128,8,128]{1,3,2,0:T(8,128)S(1)} %fusion.20), kind=kOutput, calls=%fused_computation.48 | convolution fusion | flops 1610612736 | bytes 8912896 | tf_op jit(solution)/shard_map/tkil,tklm->kim/dot_general | solution.py:70
  329.4 48.8 %all-reduce.12.cloned.1.call-done = f32[8,128,128]{2,1,0:T(8,128)} async-done(((f32[8,128,128]{2,1,0:T(8,128)}), f32[8,128,128]{2,1,0:T(8,128)}) %all-reduce.12.cloned.1.call-update) | async-done | bytes 524304 | tf_op jit(solution)/shard_map/psum | solution.py:80
  384.3 8.9 %fusion.18 = f32[8,128,8,128]{1,3,2,0:T(8,128)S(1)} fusion(f32[8,8,128,128]{3,2,1,0:T(8,128)} %fusion.28, f32[8,128,128]{2,1,0:T(8,128)S(1)} %broadcast_divide_fusion), kind=kOutput, calls=%fused_computation.19 | convolution fusion | flops 1610612736 | bytes 8912896 | tf_op jit(solution)/shard_map/tkij,kjl->tkil/dot_general | solution.py:69
  393.2 4.8 %fusion.55 = f32[8,128,128]{2,1,0:T(8,128)} fusion(f32[8,128,8,128]{3,1,2,0:T(8,128)S(1)} %copy-done.4, f32[8,128,8,128]{1,3,2,0:T(8,128)S(1)} %fusion.18), kind=kOutput, calls=%fused_computation.49 | convolution fusion | flops 1610612736 | bytes 8912896 | tf_op jit(solution)/shard_map/tkil,tklm->kim/dot_general | solution.py:70
  398.7 48.2 %all-reduce.14.cloned.1.call-done = f32[8,128,128]{2,1,0:T(8,128)} async-done(((f32[8,128,128]{2,1,0:T(8,128)}), f32[8,128,128]{2,1,0:T(8,128)}) %all-reduce.14.cloned.1.call-update) | async-done | bytes 524304 | tf_op jit(solution)/shard_map/psum | solution.py:80
  (61 shorter events, 37.0 us)
Async XLA Ops:
  7.2 11.1 %copy-start.11 = (f32[1,8,128,128]{3,2,1,0:T(8,128)S(1)}, f32[1,8,128,128]{3,2,1,0:T(8,128)}, u32[]{:S(2)}) copy-start(f32[1,8,128,128]{3,2,1,0:T(8,128)} %param.6) | copy-start | bytes 1572868
  7.2 17.2 %copy-start.12 = (s32[1,2,8]{2,1,0:T(2,128)S(1)}, s32[1,2,8]{2,1,0:T(2,128)}, u32[]{:S(2)}) copy-start(s32[1,2,8]{2,1,0:T(2,128)} %param.9) | copy-start | bytes 196
  7.2 17.3 %copy-start.7 = (f32[1,8,128,128]{3,2,1,0:T(8,128)S(1)}, f32[1,8,128,128]{3,2,1,0:T(8,128)}, u32[]{:S(2)}) copy-start(f32[1,8,128,128]{3,2,1,0:T(8,128)} %param.5) | copy-start | bytes 1572868
  7.2 166.1 %all-reduce.6.cloned.1.call-start = ((), (), s32[]{:S(2)}) async-start(), calls=%async_computation | async-start | bytes 1048576 | tf_op jit(solution)/shard_map/psum | solution.py:80
  12.7 50.1 %collective-permute-start.1 = (f32[8,8,128,128]{2,3,1,0:T(8,128)}, f32[8,8,128,128]{2,3,1,0:T(8,128)}, u32[]{:S(2)}, u32[]{:S(2)}) collective-permute-start(f32[8,8,128,128]{2,3,1,0:T(8,128)} %bitcast.173), channel_id=1, source_target_pairs={{0,4},{4,8},{8,12},{12,16},{16,20},{20,24},{24,28},{28,32},{32,36}... | collective-permute-start | bytes 12582920 | tf_op jit(solution)/shard_map/ppermute | solution.py:20
  14.6 60.2 %collective-permute-start.3 = (f32[8,8,128,128]{3,2,1,0:T(8,128)}, f32[8,8,128,128]{3,2,1,0:T(8,128)}, u32[]{:S(2)}, u32[]{:S(2)}) collective-permute-start(f32[8,8,128,128]{3,2,1,0:T(8,128)} %bitcast.174), channel_id=1, source_target_pairs={{4,0},{8,4},{12,8},{16,12},{20,16},{24,20},{28,24},{32,28},{36,32}... | collective-permute-start | bytes 12582920 | tf_op jit(solution)/shard_map/ppermute | solution.py:20
  18.6 86.6 %collective-permute-start.2 = (f32[8,128,128]{2,1,0:T(8,128)S(1)}, f32[8,128,128]{2,1,0:T(8,128)S(1)}, u32[]{:S(2)}, u32[]{:S(2)}) collective-permute-start(f32[8,128,128]{2,1,0:T(8,128)S(1)} %fusion.73), channel_id=1, source_target_pairs={{4,0},{8,4},{12,8},{16,12},{20,16},{24,20},{28,24},{32,28},{36,32}... | collective-permute-start | bytes 1572872 | tf_op jit(solution)/shard_map/ppermute | solution.py:20
  22.5 59.0 %collective-permute-start = (f32[8,128,128]{2,1,0:T(8,128)S(1)}, f32[8,128,128]{2,1,0:T(8,128)S(1)}, u32[]{:S(2)}, u32[]{:S(2)}) collective-permute-start(f32[8,128,128]{2,1,0:T(8,128)S(1)} %fusion.73), channel_id=1, source_target_pairs={{0,4},{4,8},{8,12},{12,16},{16,20},{20,24},{24,28},{28,32},{32,36}... | collective-permute-start | bytes 1572872 | tf_op jit(solution)/shard_map/ppermute | solution.py:20
  74.8 6.7 %copy-start.6 = (f32[8,8,128,128]{2,3,1,0:T(8,128)S(1)}, f32[8,8,128,128]{2,3,1,0:T(8,128)}, u32[]{:S(2)}) copy-start(f32[8,8,128,128]{2,3,1,0:T(8,128)} %broadcast_select_fusion.1) | copy-start | bytes 12582916
  74.8 6.7 %copy-start.8 = (f32[8,8,128,128]{3,2,1,0:T(8,128)S(1)}, f32[8,8,128,128]{3,2,1,0:T(8,128)}, u32[]{:S(2)}) copy-start(f32[8,8,128,128]{3,2,1,0:T(8,128)} %copy.9) | copy-start | bytes 12582916
  96.1 9.1 %copy-start.5 = (f32[8,8,128,128]{3,2,1,0:T(8,128)S(1)}, f32[8,8,128,128]{3,2,1,0:T(8,128)}, u32[]{:S(2)}) copy-start(f32[8,8,128,128]{3,2,1,0:T(8,128)} %broadcast_select_fusion) | copy-start | bytes 12582916
  96.1 9.1 %copy-start.9 = (f32[8,8,128,128]{2,3,1,0:T(8,128)S(1)}, f32[8,8,128,128]{2,3,1,0:T(8,128)}, u32[]{:S(2)}) copy-start(f32[8,8,128,128]{2,3,1,0:T(8,128)} %copy.10) | copy-start | bytes 12582916
  113.9 2.0 copy-start
  121.2 119.8 %all-reduce.8.cloned.1.call-start = ((), (), s32[]{:S(2)}) async-start(), calls=%async_computation.1 | async-start | bytes 1048576 | tf_op jit(solution)/shard_map/psum | solution.py:80
  178.3 8.9 %copy-start.1 = (f32[8,128,8,128]{3,1,2,0:T(8,128)S(1)}, f32[8,128,8,128]{3,1,2,0:T(8,128)}, u32[]{:S(2)}) copy-start(f32[8,128,8,128]{3,1,2,0:T(8,128)} %copy-done) | copy-start | bytes 12582916
  187.3 53.7 %copy-start.10 = (f32[8,128,128]{2,1,0:T(8,128)S(1)}, f32[8,128,128]{2,1,0:T(8,128)}, u32[]{:S(2)}) copy-start(f32[8,128,128]{2,1,0:T(8,128)} %all-reduce.6.cloned.1.call-done) | copy-start | bytes 1572868
  192.1 117.6 %all-reduce.10.cloned.1.call-start = ((), (), s32[]{:S(2)}) async-start(), calls=%async_computation.2 | async-start | bytes 1048576 | tf_op jit(solution)/shard_map/psum | solution.py:80
  247.1 8.8 %copy-start.2 = (f32[8,128,8,128]{3,1,2,0:T(8,128)S(1)}, f32[8,128,8,128]{3,1,2,0:T(8,128)}, u32[]{:S(2)}) copy-start(f32[8,128,8,128]{3,1,2,0:T(8,128)} %copy-done) | copy-start | bytes 12582916
  260.8 117.5 %all-reduce.12.cloned.1.call-start = ((), (), s32[]{:S(2)}) async-start(), calls=%async_computation.3 | async-start | bytes 1048576 | tf_op jit(solution)/shard_map/psum | solution.py:80
  315.6 8.9 %copy-start.3 = (f32[8,128,8,128]{3,1,2,0:T(8,128)S(1)}, f32[8,128,8,128]{3,1,2,0:T(8,128)}, u32[]{:S(2)}) copy-start(f32[8,128,8,128]{3,1,2,0:T(8,128)} %copy-done) | copy-start | bytes 12582916
  329.4 117.6 %all-reduce.14.cloned.1.call-start = ((), (), s32[]{:S(2)}) async-start(), calls=%async_computation.4 | async-start | bytes 1048576 | tf_op jit(solution)/shard_map/psum | solution.py:80
  384.3 8.9 %copy-start.4 = (f32[8,128,8,128]{3,1,2,0:T(8,128)S(1)}, f32[8,128,8,128]{3,1,2,0:T(8,128)}, u32[]{:S(2)}) copy-start(f32[8,128,8,128]{3,1,2,0:T(8,128)} %copy-done) | copy-start | bytes 12582916
Sparse Core Ops, SparseCore 0:
  121.3 51.9 all-reduce.5
  192.2 48.7 all-reduce.7
  260.9 48.7 all-reduce.9
  329.5 48.7 all-reduce.11
  398.2 48.7 all-reduce.13
where the time goes:
time: 461 us; the launch traced here: 458 us
  waiting for transfers between devices  284 us (62%)
  matrix products  86.9 us (19%)
  other arithmetic  32.2 us (7%)
  between operations  25.4 us (6%)
  local copies, waits for them, and re-layouts  18.5 us (4%)
  starting transfers between devices  11.6 us (3%)
    psum x5, waiting for transfers between devices, apply_whole(): return finish(lax.psum(partial_term(direction), 'term'))  247 us
    dot_general x5, matrix products, partial_term(): halfway = jnp.einsum('tkij,kjl->tkil', left_full, vector, precision=precise)  44.5 us
    ppermute x4, waiting for transfers between devices, from_behind(): lax.ppermute(value, axis, [(source, source + steps) for source in range(l...  36.8 us
    dot_general x5, matrix products, partial_term(): return jnp.einsum('tkil,tklm->kim', halfway, right_full, precision=precise)  24.4 us
    reduce_sum x9, other arithmetic, mean_dot(): return jnp.sum(first_arr * second_arr) / volume  17.2 us
    ppermute x4, starting transfers between devices, from_behind(): lax.ppermute(value, axis, [(source, source + steps) for source in range(l...  11.4 us
  transfers between devices with their start and end apart: 9, of which 6 were waited for; matrix products, arithmetic and copies ran while one was open for 9% of the time, Pallas kernels for 0%

commit v1 on v0

v1 whole, which is shorter than its diff:
```python
import functools
import math

import jax
import jax.numpy as jnp
from jax import lax
from jax.experimental import pallas as pl
from jax.experimental.pallas import tpu as pltpu
from jax.sharding import PartitionSpec as P

ITERS = 4
NVEC = ITERS + 2
twist_scale = 0.22
shrink = 1.047
epsilon = 1e-06

B = 128
HALF = 64
F32 = jnp.float32
BF16 = jnp.bfloat16

OWNED = 2
LOCAL_TERMS = 8
MATS = OWNED * LOCAL_TERMS
DIAG_ROW = MATS * HALF
MSG_ROWS = DIAG_ROW + MATS // 2


def split(value):
    high = value.astype(BF16)
    low = (value - high.astype(F32)).astype(BF16)
    return high, low


def dot(left, right):
    return jnp.dot(left, right, preferred_element_type=F32)


def iotas(rows):
    row = lax.broadcasted_iota(jnp.int32, (rows, B), 0)
    lane = lax.broadcasted_iota(jnp.int32, (rows, B), 1)
    return row, lane


def swap_halves(value):
    return pltpu.roll(value, HALF, 1)


def dress_kernel(segments, place_ref, left_ref, right_ref, raw_ref, alpha_ref, beta_ref):
    step = pl.program_id(0)
    seg = place_ref[0]
    odd = lax.rem(seg, 2) == 1
    edge = jnp.logical_or(seg == 0, seg == segments - 1)
    alpha_left = jnp.logical_xor(odd, edge)
    beta_left = jnp.logical_not(odd)

    raw = raw_ref[0, 0]
    skew = (raw - raw.T) * (twist_scale / math.sqrt(2.0 * B) / shrink)
    row, lane = iotas(B)
    eye = jnp.where(row == lane, 1.0, 0.0).astype(F32)
    sign = jnp.where(odd, 1.0, -1.0).astype(F32)
    diag_a = jnp.where(edge, 1.0, 1.0 / shrink).astype(F32)
    skew_a = jnp.where(edge, 0.0, sign).astype(F32)

    def factors(diag, coef):
        even, odd_part = eye * diag, skew * coef
        high, low = split((even + odd_part) * 0.5)
        right_op = jnp.concatenate([jnp.concatenate([high, low], 1)] * 2, 0)
        high, low = split(even - odd_part)
        left_op = jnp.concatenate([jnp.concatenate([high] * 2, 1), jnp.concatenate([low] * 2, 1)], 0)
        return left_op, right_op

    row_h, lane_h = iotas(HALF)
    keep_top = jnp.logical_or(lane_h >= HALF, lane_h >= row_h)
    on_diag_high = lane_h - HALF == row_h
    on_diag_low = lane_h == row_h

    for take_left, ops, out_ref in (
        (alpha_left, factors(diag_a, skew_a), alpha_ref),
        (beta_left, factors(F32(1.0 / shrink), -sign), beta_ref),
    ):
        left_op, right_op = ops
        for pair in range(2):
            rows = []
            for j in range(2):
                term = 2 * pair + j
                env = jnp.where(take_left, left_ref[0, term, 0], right_ref[0, term, 0])
                high, low = split(env + env.T)
                rows.append(jnp.concatenate([high, low], 1))
            part = dot(jnp.concatenate(rows, 0), right_op)
            high, low = split(part[:, :B] + part[:, B:])
            right_side = jnp.concatenate(
                [jnp.concatenate([high[:B], high[B:]], 1), jnp.concatenate([low[:B], low[B:]], 1)], 0
            )
            full = dot(left_op, right_side)
            full = full[:B] + full[B:]
            diag = jnp.zeros((HALF, B), F32)
            for j in range(2):
                mat = full[:, j * B : (j + 1) * B]
                top, bottom = mat[:HALF], mat[HALF:]
                turned = swap_halves(bottom)
                start = pl.multiple_of((step * 4 + 2 * pair + j) * HALF, HALF)
                out_ref[pl.ds(start, HALF), :] = jnp.where(keep_top, top, turned)
                if j == 0:
                    diag = jnp.where(on_diag_high, bottom, diag)
                else:
                    diag = jnp.where(on_diag_low, turned, diag)
            out_ref[pl.ds(DIAG_ROW + step * 2 + pair, 1), :] = jnp.sum(diag, axis=0, keepdims=True)


def dress(place, left_env, right_env, raw, offset, segments, groups):
    def env_map(step, place):
        sector = OWNED * lax.rem(place[1] + offset, groups) + step // 2
        return (0, lax.rem(step, 2), sector, 0, 0)

    def raw_map(step, place):
        return (0, OWNED * lax.rem(place[1] + offset, groups) + step // 2, 0, 0)

    out = jax.ShapeDtypeStruct((MSG_ROWS, B), F32)
    whole = pl.BlockSpec((MSG_ROWS, B), lambda step, place: (0, 0))
    return pl.pallas_call(
        functools.partial(dress_kernel, segments),
        out_shape=(out, out),
        grid_spec=pltpu.PrefetchScalarGridSpec(
            num_scalar_prefetch=1,
            grid=(4,),
            in_specs=[
                pl.BlockSpec((1, 4, 1, B, B), env_map),
                pl.BlockSpec((1, 4, 1, B, B), env_map),
                pl.BlockSpec((1, 1, B, B), raw_map),
            ],
            out_specs=(whole, whole),
        ),
        compiler_params=pltpu.CompilerParams(
            dimension_semantics=("arbitrary",), vmem_limit_bytes=24 << 20
        ),
        cost_estimate=pl.CostEstimate(flops=32 * 4 * 2 * B**3 * 2, bytes_accessed=5 << 20, transcendentals=0),
        name="dress",
    )(place, left_env, right_env, raw)


def total(value):
    tiles = jnp.sum(value.reshape(OWNED * B // 8, 8, B), axis=0)
    return jnp.sum(jnp.sum(tiles, axis=0, keepdims=True), axis=1, keepdims=True)


def unpack_into(msg_ref, dest_ref, group_index):
    row_h, lane_h = iotas(HALF)
    keep_top = jnp.logical_or(lane_h >= HALF, lane_h >= row_h)
    keep_bottom = jnp.logical_and(lane_h >= HALF, lane_h - HALF < row_h)
    on_diag = lane_h - HALF == row_h

    def body(pair, carry):
        diag_row = msg_ref[pl.ds(DIAG_ROW + pair, 1), :]
        for j in range(2):
            mat = 2 * pair + j
            packed = msg_ref[pl.ds(pl.multiple_of(mat * HALF, HALF), HALF), :]
            turned = swap_halves(packed)
            flipped = jnp.concatenate([packed, turned], 0).T
            diag = diag_row if j == 0 else swap_halves(diag_row)
            top = jnp.where(keep_top, packed, flipped[:HALF])
            bottom = jnp.where(keep_bottom, turned, flipped[HALF:])
            bottom = jnp.where(on_diag, jnp.broadcast_to(diag, (HALF, B)), bottom)
            high, low = split(jnp.concatenate([top, bottom], 0))
            owned, term = mat // LOCAL_TERMS, lax.rem(mat, LOCAL_TERMS)
            start = (owned * 4 * LOCAL_TERMS + group_index * LOCAL_TERMS + term) * B
            dest_ref[pl.ds(pl.multiple_of(start, B), B), :] = jnp.concatenate([high, low], 1)
        return carry

    lax.fori_loop(0, MATS // 2, body, 0)


def krylov_kernel(place_ref, sizes_ref, psi_ref, *refs):
    alphas, betas = refs[0:4], refs[4:8]
    basis_ref, report_ref = refs[8:10]
    left_ref, right_ref, vec_ref, acc_ref, mask_ref = refs[10:]
    odd = lax.rem(place_ref[0], 2) == 1
    group = place_ref[1]
    for d in range(4):
        unpack_into(alphas[d], left_ref, d)
        unpack_into(betas[d], right_ref, d)

    row, lane = iotas(B)
    starts = []
    for owned in range(OWNED):
        rows_live = sizes_ref[0, 0, OWNED * group + owned]
        cols_live = sizes_ref[0, 1, OWNED * group + owned]
        first = jnp.where(odd, cols_live, rows_live)
        second = jnp.where(odd, rows_live, cols_live)
        live = jnp.logical_and(row < first, lane < second)
        mask_ref[owned] = jnp.where(live, 1.0, 0.0).astype(F32)
        guess = psi_ref[0, owned]
        starts.append(jnp.where(odd, guess.T, guess))
    vector = jnp.stack(starts, 0) * mask_ref[...]

    pairs = 4 * LOCAL_TERMS // 2
    span = pairs * 2 * B

    def apply_ham():
        acc_ref[...] = jnp.zeros_like(acc_ref)

        def body(chunk, carry):
            for owned in range(OWNED):
                parts = []
                for sub in range(2):
                    start = owned * span + (chunk * 2 + sub) * 2 * B
                    start = pl.multiple_of(start, 2 * B)
                    half = dot(left_ref[pl.ds(start, 2 * B), :], vec_ref[owned])
                    high, low = split(half[:, :B] + half[:, B:])
                    mid = jnp.concatenate(
                        [jnp.concatenate([high[:B], high[B:]], 1), jnp.concatenate([low[:B], low[B:]], 1)], 0
                    )
                    out = dot(mid, right_ref[pl.ds(start, 2 * B), :])
                    parts.append((out[:B, :B] + out[:B, B:]) + (out[B:, :B] + out[B:, B:]))
                acc_ref[owned] += parts[0] + parts[1]
            return carry

        lax.fori_loop(0, pairs // 2, body, 0)
        return acc_ref[...] * mask_ref[...]

    def inverse_norm(square):
        return jnp.where(square > 0.0, lax.rsqrt(jnp.where(square > 0.0, square, 1.0)), 0.0)

    lane_1 = lax.broadcasted_iota(jnp.int32, (1, B), 1)
    report = jnp.zeros((1, B), F32)
    slot = 0

    def put(report, slot, value):
        return jnp.where(lane_1 == slot, value, report)

    grams = []
    square = total(vector * vector)
    scale = inverse_norm(square)
    report = put(report, 0, square * scale)
    basis_ref[0] = vector * scale
    previous_beta = None
    for step in range(NVEC - 1):
        current = basis_ref[step]
        for owned in range(OWNED):
            high, low = split(current[owned])
            vec_ref[owned] = jnp.concatenate([jnp.concatenate([high, low], 1)] * 2, 0)
        image = apply_ham()
        alpha = total(current * image)
        rest = image - alpha * current
        if step:
            rest = rest - previous_beta * basis_ref[step - 1]
        square = total(rest * rest)
        scale = inverse_norm(square)
        beta = square * scale
        basis_ref[step + 1] = rest * scale
        report = put(report, 1 + step, alpha)
        report = put(report, 1 + (NVEC - 1) + step, beta)
        previous_beta = beta
    slot = 1 + 2 * (NVEC - 1)
    for i in range(NVEC):
        for j in range(i, NVEC):
            report = put(report, slot, total(basis_ref[i] * basis_ref[j]))
            slot += 1
    row_8, _ = iotas(8)
    report_ref[...] = jnp.where(row_8 == group, jnp.broadcast_to(report, (8, B)), 0.0)


def krylov(place, sizes, psi, alphas, betas):
    message = pl.BlockSpec((MSG_ROWS, B), lambda i, place: (0, 0))
    return pl.pallas_call(
        krylov_kernel,
        out_shape=(
            jax.ShapeDtypeStruct((NVEC, OWNED, B, B), F32),
            jax.ShapeDtypeStruct((8, B), F32),
        ),
        grid_spec=pltpu.PrefetchScalarGridSpec(
            num_scalar_prefetch=1,
            grid=(1,),
            in_specs=[
                pl.BlockSpec(memory_space=pltpu.SMEM),
                pl.BlockSpec((1, OWNED, B, B), lambda i, place: (0, place[1], 0, 0)),
            ]
            + [message] * 8,
            out_specs=(
                pl.BlockSpec((NVEC, OWNED, B, B), lambda i, place: (0, 0, 0, 0)),
                pl.BlockSpec((8, B), lambda i, place: (0, 0)),
            ),
            scratch_shapes=[
                pltpu.VMEM((OWNED * 4 * LOCAL_TERMS * B, 2 * B), BF16),
                pltpu.VMEM((OWNED * 4 * LOCAL_TERMS * B, 2 * B), BF16),
                pltpu.VMEM((OWNED, 2 * B, 2 * B), BF16),
                pltpu.VMEM((OWNED, B, B), F32),
                pltpu.VMEM((OWNED, B, B), F32),
            ],
        ),
        compiler_params=pltpu.CompilerParams(
            dimension_semantics=("arbitrary",), vmem_limit_bytes=40 << 20
        ),
        cost_estimate=pl.CostEstimate(
            flops=5 * 128 * 4 * 2 * B**3, bytes_accessed=6 << 20, transcendentals=0
        ),
        name="krylov",
    )(place, sizes, psi, *alphas, *betas)


def davidson_kernel(volume, place_ref, report_ref, basis_ref, out_ref, energy_ref):
    odd = lax.rem(place_ref[0], 2) == 1
    group = place_ref[1]
    report = report_ref[...]
    row_8, lane_8 = iotas(8)

    def column(slot):
        return jnp.sum(jnp.where(lane_8 == slot, report, 0.0), axis=1, keepdims=True)

    weight = column(0)
    alphas = [column(1 + i) for i in range(NVEC - 1)]
    betas = [column(NVEC + i) for i in range(NVEC - 1)]
    gram = {}
    slot = 1 + 2 * (NVEC - 1)
    for i in range(NVEC):
        for j in range(i, NVEC):
            gram[i, j] = gram[j, i] = column(slot)
            slot += 1

    def mean_dot(first, second):
        parts = None
        for i, a in enumerate(first):
            inner = None
            for j, b in enumerate(second):
                piece = gram[i, j] * b
                inner = piece if inner is None else inner + piece
            piece = a * inner
            parts = piece if parts is None else parts + piece
        return jnp.sum(parts, axis=0, keepdims=True) / volume

    def apply_ham(vector):
        size = len(vector)
        out = []
        for i in range(size + 1):
            value = jnp.zeros((8, 1), F32)
            if i < size:
                value = value + alphas[i] * vector[i]
            if i >= 1:
                value = value + betas[i - 1] * vector[i - 1]
            if i + 1 < size:
                value = value + betas[i] * vector[i + 1]
            out.append(value)
        return out

    def combine(a, first, b, second):
        out = []
        for i in range(max(len(first), len(second))):
            value = None
            if i < len(first):
                value = a * first[i]
            if i < len(second):
                piece = b * second[i]
                value = piece if value is None else value + piece
            out.append(value)
        return out

    started = [weight]
    norm = jnp.sqrt(mean_dot(started, started) + epsilon)
    vector = [weight / norm]
    image = apply_ham(vector)
    energy = mean_dot(vector, image)
    for _ in range(ITERS):
        residual = combine(1.0, image, -energy, vector)
        norm = jnp.sqrt(mean_dot(residual, residual) + epsilon)
        along = mean_dot(residual, image) / norm
        unit = [value / norm for value in residual]
        image_unit = apply_ham(unit)
        curve = mean_dot(unit, image_unit)
        gap_half = 0.5 * (curve - energy)
        lowest = 0.5 * (curve + energy) - jnp.sqrt(gap_half * gap_half + along * along)
        coef_b = lowest - energy
        combined = jnp.sqrt(along * along + coef_b * coef_b)
        vector = combine(along / combined, vector, coef_b / combined, unit)
        image = combine(along / combined, image, coef_b / combined, image_unit)
        energy = lowest

    mine = lax.broadcasted_iota(jnp.int32, (8, 1), 0) == group
    coefs = [jnp.sum(jnp.where(mine, value, 0.0), axis=0, keepdims=True) for value in vector]
    for owned in range(OWNED):
        value = None
        for i, coef in enumerate(coefs):
            piece = coef * basis_ref[i, owned]
            value = piece if value is None else value + piece
        out_ref[0, owned] = jnp.where(odd, value.T, value)
    energy_ref[...] = jnp.broadcast_to(energy, (8, B))


def davidson(place, report, basis, volume):
    return pl.pallas_call(
        functools.partial(davidson_kernel, volume),
        out_shape=(
            jax.ShapeDtypeStruct((1, OWNED, B, B), F32),
            jax.ShapeDtypeStruct((8, B), F32),
        ),
        grid_spec=pltpu.PrefetchScalarGridSpec(
            num_scalar_prefetch=1,
            grid=(1,),
            in_specs=[
                pl.BlockSpec((8, B), lambda i, place: (0, 0)),
                pl.BlockSpec((NVEC - 1, OWNED, B, B), lambda i, place: (0, 0, 0, 0)),
            ],
            out_specs=(
                pl.BlockSpec((1, OWNED, B, B), lambda i, place: (0, 0, 0, 0)),
                pl.BlockSpec((8, B), lambda i, place: (0, 0)),
            ),
        ),
        compiler_params=pltpu.CompilerParams(dimension_semantics=("arbitrary",), vmem_limit_bytes=16 << 20),
        name="davidson",
    )(place, report, basis)


def exchange_pairs(segments, groups, partner, offset):
    return [
        (seg * groups + term, partner(seg) * groups + (term + offset) % groups)
        for seg in range(segments)
        for term in range(groups)
    ]


def local(segments, groups, psi_guess, transfer_raw, left_env, right_env, block_sizes):
    place = jnp.stack([lax.axis_index("chain"), lax.axis_index("term")]).astype(jnp.int32)

    def alpha_partner(seg):
        if seg in (0, segments - 1):
            return seg
        return seg + 1 if seg % 2 else seg - 1

    def beta_partner(seg):
        return seg ^ 1

    alphas, betas = [None] * groups, [None] * groups
    for offset in (2, 1, 3, 0):
        alpha, beta = dress(place, left_env, right_env, transfer_raw, offset, segments, groups)
        for value, partner, store in ((alpha, alpha_partner, alphas), (beta, beta_partner, betas)):
            pairs = exchange_pairs(segments, groups, partner, offset)
            store[offset] = lax.ppermute(value, ("chain", "term"), pairs)
    volume = float(psi_guess.shape[1] * B * B)
    basis, report = krylov(place, block_sizes, psi_guess, alphas, betas)
    report = lax.psum(report, "term")
    vector, energy = davidson(place, report, basis, volume)
    return vector, energy[0, :1]


def solution(mesh):
    segments, groups = mesh.shape["chain"], mesh.shape["term"]
    placed = (
        P("chain", None, None, None),
        P("chain", None, None, None),
        P("chain", "term", None, None, None),
        P("chain", "term", None, None, None),
        P("chain", None, None),
    )
    return jax.shard_map(
        functools.partial(local, segments, groups),
        mesh=mesh,
        in_specs=placed,
        out_specs=(P("chain", "term", None, None), P("chain")),
        check_vma=False,
    )
```

time: 461 us -> 128 us (0.28)
  waiting for transfers between devices: 284 us -> 28.5 us
  matrix products: 86.9 us -> 0 us
  Pallas kernels: 0 us -> 56.1 us
  other arithmetic: 32.2 us -> 0.08 us
  between operations: 25.4 us -> 0.71 us
  blocking collectives: 0 us -> 21.1 us
  local copies, waits for them, and re-layouts: 18.5 us -> 5.94 us
    psum x5 -> x0, waiting for transfers between devices: 247 us -> none  [apply_whole(): return finish(lax.psum(partial_term(direction), 'term'))]
    dot_general x14 -> x0, matrix products: 86.9 us -> none  [the longest x5 44.5 us: partial_term(): halfway = jnp.einsum('tkij,kjl->tkil', left_full, vector, precision=precise)]
    pallas_call x0 -> x6, Pallas kernels: none -> 56.1 us  [the longest x1 37.7 us: krylov(): pl.pallas_call(krylov_kernel, out_shape=(jax.ShapeDtypeStruct((NVEC, OWNE...]
    psum x0 -> x1, blocking collectives: none -> 21.1 us  [local(): report = lax.psum(report, 'term')]
    reduce_sum x10 -> x0, other arithmetic: 18 us -> none  [the longest x9 17.2 us: mean_dot(): return jnp.sum(first_arr * second_arr) / volume]
    select_n x2 -> x0, other arithmetic: 13.2 us -> none  [the longest x1 6.67 us: local(): right_sym = symmetric(jnp.where(is_last, right_env[0], from_right))]
    select_n x2 -> x0, local copies, waits for them, and re-layouts: 10.8 us -> none  [the longest x1 5.49 us: local(): left_sym = symmetric(jnp.where(is_first, left_env[0], from_left))]
    ppermute x4 -> x8, waiting for transfers between devices: 36.8 us -> 28.5 us  [local(): store[offset] = lax.ppermute(value, ('chain', 'term'), pairs)]
  transfers between devices with their start and end apart: 9 -> 8, of which waited for: 6 -> 4; matrix products, arithmetic and copies ran while one was open for 9% -> 0% of each run, Pallas kernels for 0% -> 10%
where the time goes in v1:
time: 128 us; the launch traced here: 127 us
  Pallas kernels  56.1 us (44%)
  waiting for transfers between devices  28.5 us (22%)
  blocking collectives  21.1 us (16%)
  starting transfers between devices  14.6 us (11%)
  local copies, waits for them, and re-layouts  5.94 us (5%)
    pallas_call x1, Pallas kernels, krylov(): pl.pallas_call(krylov_kernel, out_shape=(jax.ShapeDtypeStruct((NVEC, OWNE...  37.7 us
    ppermute x8, waiting for transfers between devices, local(): store[offset] = lax.ppermute(value, ('chain', 'term'), pairs)  28.5 us
    psum x1, blocking collectives, local(): report = lax.psum(report, 'term')  21.1 us
    pallas_call x4, Pallas kernels, dress(): pl.pallas_call(functools.partial(dress_kernel, segments), out_shape=(out,...  16.6 us
    ppermute x8, starting transfers between devices, local(): store[offset] = lax.ppermute(value, ('chain', 'term'), pairs)  14.6 us
    unnamed x10, local copies, waits for them, and re-layouts  5.43 us
  transfers between devices with their start and end apart: 8, of which 4 were waited for; matrix products, arithmetic and copies ran while one was open for 0% of the time, Pallas kernels for 10%

profile of v1, /device:TPU:2, one launch (start us, length us, event | category | flops | bytes accessed | tf_op | source)
XLA Modules:
  0.0 127.1 jit_solution(10875652762828423193)
XLA Ops:
  0.6 0.1 pad_add_fusion.place_ref
  0.7 2.2 %copy-done = f32[1,8,8,128,128]{4,3,2,1,0:T(8,128)S(1)} copy-done((f32[1,8,8,128,128]{4,3,2,1,0:T(8,128)S(1)}, f32[1,8,8,128,128]{4,3,2,1,0:T(8,128)}, u32[]{:S(2)}) %copy-start) | copy-done | bytes 4194328
  2.9 2.2 %copy-done.1 = f32[1,8,8,128,128]{4,3,2,1,0:T(8,128)S(1)} copy-done((f32[1,8,8,128,128]{4,3,2,1,0:T(8,128)S(1)}, f32[1,8,8,128,128]{4,3,2,1,0:T(8,128)}, u32[]{:S(2)}) %copy-start.1) | copy-done | bytes 4194328
  5.1 1.0 copy-done.2
  6.1 4.2 %dress.5 = (f32[1032,128]{1,0:T(8,128)S(1)}, f32[1032,128]{1,0:T(8,128)S(1)}) custom-call(s32[2]{0:T(128)S(1)} %pad_add_fusion.place_ref, f32[1,8,8,128,128]{4,3,2,1,0:T(8,128)S(1)} %copy-done, f32[1,8,8,128,128]{4,3,2,1,0:T(8,128)S(1)} %copy-done.1, f32[1,8,128,128]{3,2,1,0:T(8,128)S(1)} %copy-done.2), custom_call_target="tpu_custom_call" | custom-call | flops 1073741824 | bytes 5242880 | tf_op jit(solution)/shard_map/dress/pallas_call | solution.py:121
  10.3 1.1 collective-permute-start.1
  11.4 2.8 %collective-permute-start.5 = (f32[1032,128]{1,0:T(8,128)S(1)}, f32[1032,128]{1,0:T(8,128)S(1)}, u32[]{:S(2)}, u32[]{:S(2)}) collective-permute-start(f32[1032,128]{1,0:T(8,128)S(1)} %get-tuple-element.19), channel_id=1, source_target_pairs={{0,5},{1,6},{2,7},{3,4},{4,1},{5,2},{6,3},{7,0},{8,13},{9,14},{10,... | collective-permute-start | bytes 1585160 | tf_op jit(solution)/shard_map/ppermute | solution.py:436
  14.2 4.1 %dress.4 = (f32[1032,128]{1,0:T(8,128)S(1)}, f32[1032,128]{1,0:T(8,128)S(1)}) custom-call(s32[2]{0:T(128)S(1)} %pad_add_fusion.place_ref, f32[1,8,8,128,128]{4,3,2,1,0:T(8,128)S(1)} %copy-done, f32[1,8,8,128,128]{4,3,2,1,0:T(8,128)S(1)} %copy-done.1, f32[1,8,128,128]{3,2,1,0:T(8,128)S(1)} %copy-done.2), custom_call_target="tpu_custom_call" | custom-call | flops 1073741824 | bytes 5242880 | tf_op jit(solution)/shard_map/dress/pallas_call | solution.py:121
  18.3 1.9 %collective-permute-start = (f32[1032,128]{1,0:T(8,128)S(1)}, f32[1032,128]{1,0:T(8,128)S(1)}, u32[]{:S(2)}, u32[]{:S(2)}) collective-permute-start(f32[1032,128]{1,0:T(8,128)S(1)} %get-tuple-element.14), channel_id=1, source_target_pairs={{0,0},{1,1},{2,2},{3,3},{4,8},{5,9},{6,10},{7,11},{8,4},{9,5},{10,... | collective-permute-start | bytes 1585160 | tf_op jit(solution)/shard_map/ppermute | solution.py:436
  20.2 1.4 %collective-permute-start.4 = (f32[1032,128]{1,0:T(8,128)S(1)}, f32[1032,128]{1,0:T(8,128)S(1)}, u32[]{:S(2)}, u32[]{:S(2)}) collective-permute-start(f32[1032,128]{1,0:T(8,128)S(1)} %get-tuple-element.18), channel_id=1, source_target_pairs={{0,4},{1,5},{2,6},{3,7},{4,0},{5,1},{6,2},{7,3},{8,12},{9,13},{10,... | collective-permute-start | bytes 1585160 | tf_op jit(solution)/shard_map/ppermute | solution.py:436
  21.6 4.2 %dress.7 = (f32[1032,128]{1,0:T(8,128)S(1)}, f32[1032,128]{1,0:T(8,128)S(1)}) custom-call(s32[2]{0:T(128)S(1)} %pad_add_fusion.place_ref, f32[1,8,8,128,128]{4,3,2,1,0:T(8,128)S(1)} %copy-done, f32[1,8,8,128,128]{4,3,2,1,0:T(8,128)S(1)} %copy-done.1, f32[1,8,128,128]{3,2,1,0:T(8,128)S(1)} %copy-done.2), custom_call_target="tpu_custom_call" | custom-call | flops 1073741824 | bytes 5242880 | tf_op jit(solution)/shard_map/dress/pallas_call | solution.py:121
  25.8 1.6 %collective-permute-start.3 = (f32[1032,128]{1,0:T(8,128)S(1)}, f32[1032,128]{1,0:T(8,128)S(1)}, u32[]{:S(2)}, u32[]{:S(2)}) collective-permute-start(f32[1032,128]{1,0:T(8,128)S(1)} %get-tuple-element.17), channel_id=1, source_target_pairs={{0,3},{1,0},{2,1},{3,2},{4,11},{5,8},{6,9},{7,10},{8,7},{9,4},{10,... | collective-permute-start | bytes 1585160 | tf_op jit(solution)/shard_map/ppermute | solution.py:436
  27.4 4.2 %dress.6 = (f32[1032,128]{1,0:T(8,128)S(1)}, f32[1032,128]{1,0:T(8,128)S(1)}) custom-call(s32[2]{0:T(128)S(1)} %pad_add_fusion.place_ref, f32[1,8,8,128,128]{4,3,2,1,0:T(8,128)S(1)} %copy-done, f32[1,8,8,128,128]{4,3,2,1,0:T(8,128)S(1)} %copy-done.1, f32[1,8,128,128]{3,2,1,0:T(8,128)S(1)} %copy-done.2), custom_call_target="tpu_custom_call" | custom-call | flops 1073741824 | bytes 5242880 | tf_op jit(solution)/shard_map/dress/pallas_call | solution.py:121
  31.6 1.6 %collective-permute-start.7 = (f32[1032,128]{1,0:T(8,128)S(1)}, f32[1032,128]{1,0:T(8,128)S(1)}, u32[]{:S(2)}, u32[]{:S(2)}) collective-permute-start(f32[1032,128]{1,0:T(8,128)S(1)} %get-tuple-element.21), channel_id=1, source_target_pairs={{0,7},{1,4},{2,5},{3,6},{4,3},{5,0},{6,1},{7,2},{8,15},{9,12},{10,... | collective-permute-start | bytes 1585160 | tf_op jit(solution)/shard_map/ppermute | solution.py:436
  33.2 4.8 %collective-permute-done.5.refs_5_ = f32[1032,128]{1,0:T(8,128)S(1)} collective-permute-done((f32[1032,128]{1,0:T(8,128)S(1)}, f32[1032,128]{1,0:T(8,128)S(1)}, u32[]{:S(2)}, u32[]{:S(2)}) %collective-permute-start.5) | collective-permute-done | bytes 528416 | tf_op jit(solution)/shard_map/ppermute | solution.py:436
  38.0 1.5 %collective-permute-start.2 = (f32[1032,128]{1,0:T(8,128)S(1)}, f32[1032,128]{1,0:T(8,128)S(1)}, u32[]{:S(2)}, u32[]{:S(2)}) collective-permute-start(f32[1032,128]{1,0:T(8,128)S(1)} %get-tuple-element.16), channel_id=1, source_target_pairs={{0,2},{1,3},{2,0},{3,1},{4,10},{5,11},{6,8},{7,9},{8,6},{9,7},{10,... | collective-permute-start | bytes 1585160 | tf_op jit(solution)/shard_map/ppermute | solution.py:436
  39.5 2.7 %collective-permute-start.6 = (f32[1032,128]{1,0:T(8,128)S(1)}, f32[1032,128]{1,0:T(8,128)S(1)}, u32[]{:S(2)}, u32[]{:S(2)}) collective-permute-start(f32[1032,128]{1,0:T(8,128)S(1)} %get-tuple-element.20), channel_id=1, source_target_pairs={{0,6},{1,7},{2,4},{3,5},{4,2},{5,3},{6,0},{7,1},{8,14},{9,15},{10,... | collective-permute-start | bytes 1585160 | tf_op jit(solution)/shard_map/ppermute | solution.py:436
  42.2 0.6 collective-permute-done.3.refs_3_
  42.8 22.5 %collective-permute-done.7.refs_7_ = f32[1032,128]{1,0:T(8,128)S(1)} collective-permute-done((f32[1032,128]{1,0:T(8,128)S(1)}, f32[1032,128]{1,0:T(8,128)S(1)}, u32[]{:S(2)}, u32[]{:S(2)}) %collective-permute-start.7) | collective-permute-done | bytes 528416 | tf_op jit(solution)/shard_map/ppermute | solution.py:436
  65.3 0.6 collective-permute-done.6.refs_6_
  66.0 37.7 %krylov.1 = (f32[6,2,128,128]{3,2,1,0:T(8,128)S(1)}, f32[8,128]{1,0:T(8,128)S(1)}) custom-call(s32[2]{0:T(128)S(1)} %pad_add_fusion.place_ref, s32[1,2,8]{2,1,0:T(2,128)S(1)} %copy-done.4, f32[1,8,128,128]{3,2,1,0:T(8,128)S(1)} %copy-done.3, f32[1032,128]{1,0:T(8,128)S(1)} %collective-permute-done.refs_0_, f32[1032,128]{1,0:T(8,128)S(1)} %collective-permute-done.1.refs_1_, ...), custom_call_target="tpu_custom_call" | custom-call | flops 10737418240 | bytes 6291456 | tf_op jit(solution)/shard_map/krylov/pallas_call | solution.py:265
  103.7 21.1 %psum.7.report_ref = f32[8,128]{1,0:T(8,128)S(1)} all-reduce(f32[8,128]{1,0:T(8,128)S(1)} %get-tuple-element.22), channel_id=1, replica_groups=mesh['chain'=64,'term'=4] {'term'}, use_global_device_ids=true, to_apply=%region_0.0 | all-reduce | flops 1024 | bytes 8192 | tf_op jit(solution)/shard_map/psum | solution.py:439
  124.8 1.8 %davidson.1 = (f32[1,2,128,128]{3,2,1,0:T(8,128)}, f32[8,128]{1,0:T(8,128)S(1)}) custom-call(s32[2]{0:T(128)S(1)} %pad_add_fusion.place_ref, f32[8,128]{1,0:T(8,128)S(1)} %psum.7.report_ref, f32[6,2,128,128]{3,2,1,0:T(8,128)S(1)} %get-tuple-element.23.basis_ref), custom_call_target="tpu_custom_call" | custom-call | tf_op jit(solution)/shard_map/davidson/pallas_call | solution.py:389
  126.6 0.5 slice.3
  (11 shorter events, 0.0 us)
Async XLA Ops:
  0.7 2.2 %copy-start = (f32[1,8,8,128,128]{4,3,2,1,0:T(8,128)S(1)}, f32[1,8,8,128,128]{4,3,2,1,0:T(8,128)}, u32[]{:S(2)}) copy-start(f32[1,8,8,128,128]{4,3,2,1,0:T(8,128)} %left_ref.7) | copy-start | bytes 12582916
  2.9 2.2 %copy-start.1 = (f32[1,8,8,128,128]{4,3,2,1,0:T(8,128)S(1)}, f32[1,8,8,128,128]{4,3,2,1,0:T(8,128)}, u32[]{:S(2)}) copy-start(f32[1,8,8,128,128]{4,3,2,1,0:T(8,128)} %right_ref.7) | copy-start | bytes 12582916
  5.1 1.0 copy-start.2
  10.3 21.3 %collective-permute-start.1 = (f32[1032,128]{1,0:T(8,128)S(1)}, f32[1032,128]{1,0:T(8,128)S(1)}, u32[]{:S(2)}, u32[]{:S(2)}) collective-permute-start(f32[1032,128]{1,0:T(8,128)S(1)} %get-tuple-element.15), channel_id=1, source_target_pairs={{0,1},{1,2},{2,3},{3,0},{4,9},{5,10},{6,11},{7,8},{8,5},{9,6},{10,... | collective-permute-start | bytes 1585160 | tf_op jit(solution)/shard_map/ppermute | solution.py:436
  11.4 26.7 %collective-permute-start.5 = (f32[1032,128]{1,0:T(8,128)S(1)}, f32[1032,128]{1,0:T(8,128)S(1)}, u32[]{:S(2)}, u32[]{:S(2)}) collective-permute-start(f32[1032,128]{1,0:T(8,128)S(1)} %get-tuple-element.19), channel_id=1, source_target_pairs={{0,5},{1,6},{2,7},{3,4},{4,1},{5,2},{6,3},{7,0},{8,13},{9,14},{10,... | collective-permute-start | bytes 1585160 | tf_op jit(solution)/shard_map/ppermute | solution.py:436
  18.3 21.2 %collective-permute-start = (f32[1032,128]{1,0:T(8,128)S(1)}, f32[1032,128]{1,0:T(8,128)S(1)}, u32[]{:S(2)}, u32[]{:S(2)}) collective-permute-start(f32[1032,128]{1,0:T(8,128)S(1)} %get-tuple-element.14), channel_id=1, source_target_pairs={{0,0},{1,1},{2,2},{3,3},{4,8},{5,9},{6,10},{7,11},{8,4},{9,5},{10,... | collective-permute-start | bytes 1585160 | tf_op jit(solution)/shard_map/ppermute | solution.py:436
  20.2 22.0 %collective-permute-start.4 = (f32[1032,128]{1,0:T(8,128)S(1)}, f32[1032,128]{1,0:T(8,128)S(1)}, u32[]{:S(2)}, u32[]{:S(2)}) collective-permute-start(f32[1032,128]{1,0:T(8,128)S(1)} %get-tuple-element.18), channel_id=1, source_target_pairs={{0,4},{1,5},{2,6},{3,7},{4,0},{5,1},{6,2},{7,3},{8,12},{9,13},{10,... | collective-permute-start | bytes 1585160 | tf_op jit(solution)/shard_map/ppermute | solution.py:436
  25.8 40.2 %copy-start.3 = (f32[1,8,128,128]{3,2,1,0:T(8,128)S(1)}, f32[1,8,128,128]{3,2,1,0:T(8,128)}, u32[]{:S(2)}) copy-start(f32[1,8,128,128]{3,2,1,0:T(8,128)} %psi_ref.1) | copy-start | bytes 1572868
  25.8 40.2 %copy-start.4 = (s32[1,2,8]{2,1,0:T(2,128)S(1)}, s32[1,2,8]{2,1,0:T(2,128)}, u32[]{:S(2)}) copy-start(s32[1,2,8]{2,1,0:T(2,128)} %sizes_ref.1) | copy-start | bytes 196
  25.8 17.0 %collective-permute-start.3 = (f32[1032,128]{1,0:T(8,128)S(1)}, f32[1032,128]{1,0:T(8,128)S(1)}, u32[]{:S(2)}, u32[]{:S(2)}) collective-permute-start(f32[1032,128]{1,0:T(8,128)S(1)} %get-tuple-element.17), channel_id=1, source_target_pairs={{0,3},{1,0},{2,1},{3,2},{4,11},{5,8},{6,9},{7,10},{8,7},{9,4},{10,... | collective-permute-start | bytes 1585160 | tf_op jit(solution)/shard_map/ppermute | solution.py:436
  31.6 33.7 %collective-permute-start.7 = (f32[1032,128]{1,0:T(8,128)S(1)}, f32[1032,128]{1,0:T(8,128)S(1)}, u32[]{:S(2)}, u32[]{:S(2)}) collective-permute-start(f32[1032,128]{1,0:T(8,128)S(1)} %get-tuple-element.21), channel_id=1, source_target_pairs={{0,7},{1,4},{2,5},{3,6},{4,3},{5,0},{6,1},{7,2},{8,15},{9,12},{10,... | collective-permute-start | bytes 1585160 | tf_op jit(solution)/shard_map/ppermute | solution.py:436
  38.0 27.3 %collective-permute-start.2 = (f32[1032,128]{1,0:T(8,128)S(1)}, f32[1032,128]{1,0:T(8,128)S(1)}, u32[]{:S(2)}, u32[]{:S(2)}) collective-permute-start(f32[1032,128]{1,0:T(8,128)S(1)} %get-tuple-element.16), channel_id=1, source_target_pairs={{0,2},{1,3},{2,0},{3,1},{4,10},{5,11},{6,8},{7,9},{8,6},{9,7},{10,... | collective-permute-start | bytes 1585160 | tf_op jit(solution)/shard_map/ppermute | solution.py:436
  39.5 26.5 %collective-permute-start.6 = (f32[1032,128]{1,0:T(8,128)S(1)}, f32[1032,128]{1,0:T(8,128)S(1)}, u32[]{:S(2)}, u32[]{:S(2)}) collective-permute-start(f32[1032,128]{1,0:T(8,128)S(1)} %get-tuple-element.20), channel_id=1, source_target_pairs={{0,6},{1,7},{2,4},{3,5},{4,2},{5,3},{6,0},{7,1},{8,14},{9,15},{10,... | collective-permute-start | bytes 1585160 | tf_op jit(solution)/shard_map/ppermute | solution.py:436

commit v2 on v1

--- a/solution.py
+++ b/solution.py
@@ -75,37 +75,42 @@
     on_diag_high = lane_h - HALF == row_h
     on_diag_low = lane_h == row_h
 
-    for take_left, ops, out_ref in (
+    sides = (
         (alpha_left, factors(diag_a, skew_a), alpha_ref),
         (beta_left, factors(F32(1.0 / shrink), -sign), beta_ref),
-    ):
-        left_op, right_op = ops
-        for pair in range(2):
-            rows = []
-            for j in range(2):
-                term = 2 * pair + j
-                env = jnp.where(take_left, left_ref[0, term, 0], right_ref[0, term, 0])
-                high, low = split(env + env.T)
-                rows.append(jnp.concatenate([high, low], 1))
-            part = dot(jnp.concatenate(rows, 0), right_op)
-            high, low = split(part[:, :B] + part[:, B:])
-            right_side = jnp.concatenate(
-                [jnp.concatenate([high[:B], high[B:]], 1), jnp.concatenate([low[:B], low[B:]], 1)], 0
-            )
-            full = dot(left_op, right_side)
-            full = full[:B] + full[B:]
-            diag = jnp.zeros((HALF, B), F32)
-            for j in range(2):
-                mat = full[:, j * B : (j + 1) * B]
-                top, bottom = mat[:HALF], mat[HALF:]
-                turned = swap_halves(bottom)
-                start = pl.multiple_of((step * 4 + 2 * pair + j) * HALF, HALF)
-                out_ref[pl.ds(start, HALF), :] = jnp.where(keep_top, top, turned)
-                if j == 0:
-                    diag = jnp.where(on_diag_high, bottom, diag)
-                else:
-                    diag = jnp.where(on_diag_low, turned, diag)
-            out_ref[pl.ds(DIAG_ROW + step * 2 + pair, 1), :] = jnp.sum(diag, axis=0, keepdims=True)
+    )
+    work = [(side, pair) for side in range(2) for pair in range(2)]
+    parts = []
+    for side, pair in work:
+        take_left, (_, right_op), _ = sides[side]
+        rows = []
+        for term in (2 * pair, 2 * pair + 1):
+            env = jnp.where(take_left, left_ref[0, term, 0], right_ref[0, term, 0])
+            high, low = split(env + env.T)
+            rows.append(jnp.concatenate([high, low], 1))
+        parts.append(dot(jnp.concatenate(rows, 0), right_op))
+    fulls = []
+    for (side, pair), part in zip(work, parts):
+        high, low = split(part[:, :B] + part[:, B:])
+        right_side = jnp.concatenate(
+            [jnp.concatenate([high[:B], high[B:]], 1), jnp.concatenate([low[:B], low[B:]], 1)], 0
+        )
+        full = dot(sides[side][1][0], right_side)
+        fulls.append(full[:B] + full[B:])
+    for (side, pair), full in zip(work, fulls):
+        out_ref = sides[side][2]
+        diag = jnp.zeros((HALF, B), F32)
+        for j in range(2):
+            mat = full[:, j * B : (j + 1) * B]
+            top, bottom = mat[:HALF], mat[HALF:]
+            turned = swap_halves(bottom)
+            start = pl.multiple_of((step * 4 + 2 * pair + j) * HALF, HALF)
+            out_ref[pl.ds(start, HALF), :] = jnp.where(keep_top, top, turned)
+            if j == 0:
+                diag = jnp.where(on_diag_high, bottom, diag)
+            else:
+                diag = jnp.where(on_diag_low, turned, diag)
+        out_ref[pl.ds(DIAG_ROW + step * 2 + pair, 1), :] = jnp.sum(diag, axis=0, keepdims=True)
 
 
 def dress(place, left_env, right_env, raw, offset, segments, groups):
@@ -132,9 +137,9 @@
             out_specs=(whole, whole),
         ),
         compiler_params=pltpu.CompilerParams(
-            dimension_semantics=("arbitrary",), vmem_limit_bytes=24 << 20
-        ),
-        cost_estimate=pl.CostEstimate(flops=32 * 4 * 2 * B**3 * 2, bytes_accessed=5 << 20, transcendentals=0),
+            dimension_semantics=("arbitrary",), vmem_limit_bytes=58 << 20
+        ),
+        cost_estimate=pl.CostEstimate(flops=1000, bytes_accessed=1000, transcendentals=0),
         name="dress",
     )(place, left_env, right_env, raw)
 
@@ -144,78 +149,133 @@
     return jnp.sum(jnp.sum(tiles, axis=0, keepdims=True), axis=1, keepdims=True)
 
 
-def unpack_into(msg_ref, dest_ref, group_index):
+def unpack(msg_ref, pairs):
     row_h, lane_h = iotas(HALF)
     keep_top = jnp.logical_or(lane_h >= HALF, lane_h >= row_h)
     keep_bottom = jnp.logical_and(lane_h >= HALF, lane_h - HALF < row_h)
     on_diag = lane_h - HALF == row_h
-
-    def body(pair, carry):
-        diag_row = msg_ref[pl.ds(DIAG_ROW + pair, 1), :]
+    packed = [msg_ref[2 * pair * HALF : (2 * pair + 2) * HALF, :] for pair in pairs]
+    diags = [msg_ref[DIAG_ROW + pair : DIAG_ROW + pair + 1, :] for pair in pairs]
+    out = []
+    for pair_value, diag_row in zip(packed, diags):
         for j in range(2):
-            mat = 2 * pair + j
-            packed = msg_ref[pl.ds(pl.multiple_of(mat * HALF, HALF), HALF), :]
-            turned = swap_halves(packed)
-            flipped = jnp.concatenate([packed, turned], 0).T
+            value = pair_value[j * HALF : (j + 1) * HALF]
+            turned = swap_halves(value)
+            flipped = jnp.concatenate([value, turned], 0).T
             diag = diag_row if j == 0 else swap_halves(diag_row)
-            top = jnp.where(keep_top, packed, flipped[:HALF])
+            top = jnp.where(keep_top, value, flipped[:HALF])
             bottom = jnp.where(keep_bottom, turned, flipped[HALF:])
             bottom = jnp.where(on_diag, jnp.broadcast_to(diag, (HALF, B)), bottom)
             high, low = split(jnp.concatenate([top, bottom], 0))
-            owned, term = mat // LOCAL_TERMS, lax.rem(mat, LOCAL_TERMS)
-            start = (owned * 4 * LOCAL_TERMS + group_index * LOCAL_TERMS + term) * B
-            dest_ref[pl.ds(pl.multiple_of(start, B), B), :] = jnp.concatenate([high, low], 1)
-        return carry
-
-    lax.fori_loop(0, MATS // 2, body, 0)
+            out.append(jnp.concatenate([high, low], 1))
+    return out
+
+
+def doubled(vector):
+    high, low = split(vector)
+    return jnp.concatenate([jnp.concatenate([high, low], 1)] * 2, 0)
+
+
+def between(half):
+    high, low = split(half[:, :B] + half[:, B:])
+    return jnp.concatenate(
+        [jnp.concatenate([high[:B], high[B:]], 1), jnp.concatenate([low[:B], low[B:]], 1)], 0
+    )
+
+
+def quarters(out):
+    return (out[:B, :B] + out[:B, B:]) + (out[B:, :B] + out[B:, B:])
+
+
+def live_mask(place_ref, sizes_ref, owned):
+    odd = lax.rem(place_ref[0], 2) == 1
+    row, lane = iotas(B)
+    rows_live = sizes_ref[0, 0, OWNED * place_ref[1] + owned]
+    cols_live = sizes_ref[0, 1, OWNED * place_ref[1] + owned]
+    first = jnp.where(odd, cols_live, rows_live)
+    second = jnp.where(odd, rows_live, cols_live)
+    return jnp.where(jnp.logical_and(row < first, lane < second), 1.0, 0.0).astype(F32)
+
+
+def start_vector(place_ref, sizes_ref, psi_ref, owned):
+    odd = lax.rem(place_ref[0], 2) == 1
+    guess = psi_ref[0, owned]
+    return jnp.where(odd, guess.T, guess) * live_mask(place_ref, sizes_ref, owned)
+
+
+def arrive_kernel(place_ref, sizes_ref, psi_ref, before_ref, alpha_ref, beta_ref, left_ref, right_ref, image_ref):
+    per_sector = LOCAL_TERMS // 2
+    for owned in range(OWNED):
+        vector = doubled(start_vector(place_ref, sizes_ref, psi_ref, owned))
+        pairs = [owned * per_sector + i for i in range(per_sector)]
+        lefts = unpack(alpha_ref, pairs)
+        rights = unpack(beta_ref, pairs)
+        for i in range(LOCAL_TERMS):
+            start = (owned * LOCAL_TERMS + i) * B
+            left_ref[start : start + B, :] = lefts[i]
+            right_ref[start : start + B, :] = rights[i]
+        mids = [between(dot(jnp.concatenate(lefts[2 * i : 2 * i + 2], 0), vector)) for i in range(per_sector)]
+        image = quarters(dot(jnp.concatenate(mids, 1), jnp.concatenate(rights, 0)))
+        image_ref[owned] = before_ref[owned] + image
+
+
+def arrive(place, sizes, psi, before, alpha, beta):
+    rows = MATS * B
+    message = pl.BlockSpec((MSG_ROWS, B), lambda i, place: (0, 0))
+    block = pl.BlockSpec((rows, 2 * B), lambda i, place: (0, 0))
+    return pl.pallas_call(
+        arrive_kernel,
+        out_shape=(
+            jax.ShapeDtypeStruct((rows, 2 * B), BF16),
+            jax.ShapeDtypeStruct((rows, 2 * B), BF16),
+            jax.ShapeDtypeStruct((OWNED, B, B), F32),
+        ),
+        grid_spec=pltpu.PrefetchScalarGridSpec(
+            num_scalar_prefetch=1,
+            grid=(1,),
+            in_specs=[
+                pl.BlockSpec(memory_space=pltpu.SMEM),
+                pl.BlockSpec((1, OWNED, B, B), lambda i, place: (0, place[1], 0, 0)),
+                pl.BlockSpec((OWNED, B, B), lambda i, place: (0, 0, 0)),
+                message,
+                message,
+            ],
+            out_specs=(block, block, pl.BlockSpec((OWNED, B, B), lambda i, place: (0, 0, 0))),
+        ),
+        compiler_params=pltpu.CompilerParams(
+            dimension_semantics=("arbitrary",), vmem_limit_bytes=20 << 20
+        ),
+        cost_estimate=pl.CostEstimate(flops=1000, bytes_accessed=1000, transcendentals=0),
+        name="arrive",
+    )(place, sizes, psi, before, alpha, beta)
 
 
 def krylov_kernel(place_ref, sizes_ref, psi_ref, *refs):
-    alphas, betas = refs[0:4], refs[4:8]
-    basis_ref, report_ref = refs[8:10]
-    left_ref, right_ref, vec_ref, acc_ref, mask_ref = refs[10:]
-    odd = lax.rem(place_ref[0], 2) == 1
+    lefts, rights, image_ref = refs[0:4], refs[4:8], refs[8]
+    basis_ref, report_ref = refs[9:11]
+    vec_ref, acc_ref, mask_ref = refs[11:]
     group = place_ref[1]
-    for d in range(4):
-        unpack_into(alphas[d], left_ref, d)
-        unpack_into(betas[d], right_ref, d)
-
-    row, lane = iotas(B)
     starts = []
     for owned in range(OWNED):
-        rows_live = sizes_ref[0, 0, OWNED * group + owned]
-        cols_live = sizes_ref[0, 1, OWNED * group + owned]
-        first = jnp.where(odd, cols_live, rows_live)
-        second = jnp.where(odd, rows_live, cols_live)
-        live = jnp.logical_and(row < first, lane < second)
-        mask_ref[owned] = jnp.where(live, 1.0, 0.0).astype(F32)
-        guess = psi_ref[0, owned]
-        starts.append(jnp.where(odd, guess.T, guess))
-    vector = jnp.stack(starts, 0) * mask_ref[...]
-
-    pairs = 4 * LOCAL_TERMS // 2
-    span = pairs * 2 * B
+        mask_ref[owned] = live_mask(place_ref, sizes_ref, owned)
+        starts.append(start_vector(place_ref, sizes_ref, psi_ref, owned))
+    vector = jnp.stack(starts, 0)
 
     def apply_ham():
         acc_ref[...] = jnp.zeros_like(acc_ref)
 
-        def body(chunk, carry):
+        def body(index, carry):
+            units = []
             for owned in range(OWNED):
-                parts = []
-                for sub in range(2):
-                    start = owned * span + (chunk * 2 + sub) * 2 * B
-                    start = pl.multiple_of(start, 2 * B)
-                    half = dot(left_ref[pl.ds(start, 2 * B), :], vec_ref[owned])
-                    high, low = split(half[:, :B] + half[:, B:])
-                    mid = jnp.concatenate(
-                        [jnp.concatenate([high[:B], high[B:]], 1), jnp.concatenate([low[:B], low[B:]], 1)], 0
-                    )
-                    out = dot(mid, right_ref[pl.ds(start, 2 * B), :])
-                    parts.append((out[:B, :B] + out[:B, B:]) + (out[B:, :B] + out[B:, B:]))
-                acc_ref[owned] += parts[0] + parts[1]
+                start = pl.multiple_of((owned * (LOCAL_TERMS // 2) + index) * 2 * B, 2 * B)
+                units.append([between(dot(left[pl.ds(start, 2 * B), :], vec_ref[owned])) for left in lefts])
+            for owned in range(OWNED):
+                start = pl.multiple_of((owned * (LOCAL_TERMS // 2) + index) * 2 * B, 2 * B)
+                right = jnp.concatenate([ref[pl.ds(start, 2 * B), :] for ref in rights], 0)
+                acc_ref[owned] += quarters(dot(jnp.concatenate(units[owned], 1), right))
             return carry
 
-        lax.fori_loop(0, pairs // 2, body, 0)
+        lax.fori_loop(0, LOCAL_TERMS // 2, body, 0)
         return acc_ref[...] * mask_ref[...]
 
     def inverse_norm(square):
@@ -223,12 +283,10 @@
 
     lane_1 = lax.broadcasted_iota(jnp.int32, (1, B), 1)
     report = jnp.zeros((1, B), F32)
-    slot = 0
 
     def put(report, slot, value):
         return jnp.where(lane_1 == slot, value, report)
 
-    grams = []
     square = total(vector * vector)
     scale = inverse_norm(square)
     report = put(report, 0, square * scale)
@@ -236,10 +294,12 @@
     previous_beta = None
     for step in range(NVEC - 1):
         current = basis_ref[step]
-        for owned in range(OWNED):
-            high, low = split(current[owned])
-            vec_ref[owned] = jnp.concatenate([jnp.concatenate([high, low], 1)] * 2, 0)
-        image = apply_ham()
+        if step:
+            for owned in range(OWNED):
+                vec_ref[owned] = doubled(current[owned])
+            image = apply_ham()
+        else:
+            image = image_ref[...] * mask_ref[...] * scale
         alpha = total(current * image)
         rest = image - alpha * current
         if step:
@@ -260,8 +320,8 @@
     report_ref[...] = jnp.where(row_8 == group, jnp.broadcast_to(report, (8, B)), 0.0)
 
 
-def krylov(place, sizes, psi, alphas, betas):
-    message = pl.BlockSpec((MSG_ROWS, B), lambda i, place: (0, 0))
+def krylov(place, sizes, psi, lefts, rights, image):
+    block = pl.BlockSpec((MATS * B, 2 * B), lambda i, place: (0, 0))
     return pl.pallas_call(
         krylov_kernel,
         out_shape=(
@@ -275,27 +335,26 @@
                 pl.BlockSpec(memory_space=pltpu.SMEM),
                 pl.BlockSpec((1, OWNED, B, B), lambda i, place: (0, place[1], 0, 0)),
             ]
-            + [message] * 8,
+            + [block] * 8
+            + [pl.BlockSpec((OWNED, B, B), lambda i, place: (0, 0, 0))],
             out_specs=(
                 pl.BlockSpec((NVEC, OWNED, B, B), lambda i, place: (0, 0, 0, 0)),
                 pl.BlockSpec((8, B), lambda i, place: (0, 0)),
             ),
             scratch_shapes=[
-                pltpu.VMEM((OWNED * 4 * LOCAL_TERMS * B, 2 * B), BF16),
-                pltpu.VMEM((OWNED * 4 * LOCAL_TERMS * B, 2 * B), BF16),
                 pltpu.VMEM((OWNED, 2 * B, 2 * B), BF16),
                 pltpu.VMEM((OWNED, B, B), F32),
                 pltpu.VMEM((OWNED, B, B), F32),
             ],
         ),
         compiler_params=pltpu.CompilerParams(
-            dimension_semantics=("arbitrary",), vmem_limit_bytes=40 << 20
+            dimension_semantics=("arbitrary",), vmem_limit_bytes=28 << 20
         ),
         cost_estimate=pl.CostEstimate(
-            flops=5 * 128 * 4 * 2 * B**3, bytes_accessed=6 << 20, transcendentals=0
+            flops=4 * 128 * 4 * 2 * B**3, bytes_accessed=9 << 20, transcendentals=0
         ),
         name="krylov",
-    )(place, sizes, psi, *alphas, *betas)
+    )(place, sizes, psi, *lefts, *rights, image)
 
 
 def davidson_kernel(volume, place_ref, report_ref, basis_ref, out_ref, energy_ref):
@@ -428,14 +487,21 @@
     def beta_partner(seg):
         return seg ^ 1
 
-    alphas, betas = [None] * groups, [None] * groups
+    messages = []
     for offset in (2, 1, 3, 0):
         alpha, beta = dress(place, left_env, right_env, transfer_raw, offset, segments, groups)
-        for value, partner, store in ((alpha, alpha_partner, alphas), (beta, beta_partner, betas)):
-            pairs = exchange_pairs(segments, groups, partner, offset)
-            store[offset] = lax.ppermute(value, ("chain", "term"), pairs)
+        alpha, beta, place = lax.optimization_barrier((alpha, beta, place))
+        messages.append((offset, alpha, beta))
+    lefts, rights = [], []
+    image = jnp.zeros((OWNED, B, B), F32)
+    for offset, alpha, beta in messages:
+        alpha = lax.ppermute(alpha, ("chain", "term"), exchange_pairs(segments, groups, alpha_partner, offset))
+        beta = lax.ppermute(beta, ("chain", "term"), exchange_pairs(segments, groups, beta_partner, offset))
+        left, right, image = arrive(place, block_sizes, psi_guess, image, alpha, beta)
+        lefts.append(left)
+        rights.append(right)
     volume = float(psi_guess.shape[1] * B * B)
-    basis, report = krylov(place, block_sizes, psi_guess, alphas, betas)
+    basis, report = krylov(place, block_sizes, psi_guess, lefts, rights, image)
     report = lax.psum(report, "term")
     vector, energy = davidson(place, report, basis, volume)
     return vector, energy[0, :1]

time: 128 us -> 93.2 us (0.73)
  waiting for transfers between devices: 28.5 us -> 15.5 us
  blocking collectives: 21.1 us -> 10.1 us
  Pallas kernels: 56.1 us -> 50.6 us
  local copies, waits for them, and re-layouts: 5.94 us -> 0.54 us
    pallas_call x1, Pallas kernels: 37.7 us -> 14.6 us  [krylov(): pl.pallas_call(krylov_kernel, out_shape=(jax.ShapeDtypeStruct((NVEC, OWNE...]
    ppermute x8, waiting for transfers between devices: 28.5 us -> 15.5 us  [the longest x4 15.5 us: local(): lax.ppermute(beta, ('chain', 'term'), exchange_pairs(segments, groups, be...]
    psum x1, blocking collectives: 21.1 us -> 10.1 us  [local(): report = lax.psum(report, 'term')]
    pallas_call x0 -> x4, Pallas kernels: none -> 10 us  [arrive(): pl.pallas_call(arrive_kernel, out_shape=(jax.ShapeDtypeStruct((rows, 2 *...]
    pallas_call x4, Pallas kernels: 16.6 us -> 24.3 us  [dress(): pl.pallas_call(functools.partial(dress_kernel, segments), out_shape=(out,...]
    unnamed x10 -> x8, local copies, waits for them, and re-layouts: 5.43 us -> 0.02 us
  transfers between devices with their start and end apart: 8 -> 8, of which waited for: 4 -> 2; matrix products, arithmetic and copies ran while one was open for 0% -> 0% of each run, Pallas kernels for 10% -> 28%
where the time goes in v2:
time: 93.2 us; the launch traced here: 92.8 us
  Pallas kernels  50.6 us (54%)
  waiting for transfers between devices  15.5 us (17%)
  starting transfers between devices  14.6 us (16%)
  blocking collectives  10.1 us (11%)
    pallas_call x4, Pallas kernels, dress(): pl.pallas_call(functools.partial(dress_kernel, segments), out_shape=(out,...  24.3 us
    ppermute x4, waiting for transfers between devices, local(): lax.ppermute(beta, ('chain', 'term'), exchange_pairs(segments, groups, be...  15.5 us
    pallas_call x1, Pallas kernels, krylov(): pl.pallas_call(krylov_kernel, out_shape=(jax.ShapeDtypeStruct((NVEC, OWNE...  14.6 us
    psum x1, blocking collectives, local(): report = lax.psum(report, 'term')  10.1 us
    pallas_call x4, Pallas kernels, arrive(): pl.pallas_call(arrive_kernel, out_shape=(jax.ShapeDtypeStruct((rows, 2 *...  10 us
    ppermute x4, starting transfers between devices, local(): lax.ppermute(beta, ('chain', 'term'), exchange_pairs(segments, groups, be...  8.03 us
    ppermute x4, starting transfers between devices, local(): lax.ppermute(alpha, ('chain', 'term'), exchange_pairs(segments, groups, a...  6.61 us
  transfers between devices with their start and end apart: 8, of which 2 were waited for; matrix products, arithmetic and copies ran while one was open for 0% of the time, Pallas kernels for 28%

profile of v2, /device:TPU:2, one launch (start us, length us, event | category | flops | bytes accessed | tf_op | source)
XLA Modules:
  0.0 92.8 jit_solution(6201476995760038140)
XLA Ops:
  0.6 0.7 pad_add_fusion.place_ref
  1.3 6.1 %dress.4 = (f32[1032,128]{1,0:T(8,128)}, f32[1032,128]{1,0:T(8,128)}) custom-call(s32[2]{0:T(128)} %pad_add_fusion.place_ref, f32[1,8,8,128,128]{4,3,2,1,0:T(8,128)} %left_ref.7, f32[1,8,8,128,128]{4,3,2,1,0:T(8,128)} %right_ref.7, f32[1,8,128,128]{3,2,1,0:T(8,128)} %raw_ref.7), custom_call_target="tpu_custom_call" | custom-call | flops 1000 | bytes 1000 | tf_op jit(solution)/shard_map/dress/pallas_call | solution.py:126
  7.3 2.6 %collective-permute-start = (f32[1032,128]{1,0:T(8,128)}, f32[1032,128]{1,0:T(8,128)S(1)}, u32[]{:S(2)}, u32[]{:S(2)}) collective-permute-start(f32[1032,128]{1,0:T(8,128)} %get-tuple-element.50), channel_id=1, source_target_pairs={{0,2},{1,3},{2,0},{3,1},{4,10},{5,11},{6,8},{7,9},{8,6},{9,7},{10,... | collective-permute-start | bytes 1585160 | tf_op jit(solution)/shard_map/ppermute | solution.py:498
  10.0 1.6 %collective-permute-start.1 = (f32[1032,128]{1,0:T(8,128)}, f32[1032,128]{1,0:T(8,128)S(1)}, u32[]{:S(2)}, u32[]{:S(2)}) collective-permute-start(f32[1032,128]{1,0:T(8,128)} %get-tuple-element.51), channel_id=1, source_target_pairs={{0,6},{1,7},{2,4},{3,5},{4,2},{5,3},{6,0},{7,1},{8,14},{9,15},{10,... | collective-permute-start | bytes 1585160 | tf_op jit(solution)/shard_map/ppermute | solution.py:499
  11.5 6.1 %dress.5 = (f32[1032,128]{1,0:T(8,128)}, f32[1032,128]{1,0:T(8,128)}) custom-call(s32[2]{0:T(128)} %pad_add_fusion.place_ref, f32[1,8,8,128,128]{4,3,2,1,0:T(8,128)} %left_ref.7, f32[1,8,8,128,128]{4,3,2,1,0:T(8,128)} %right_ref.7, f32[1,8,128,128]{3,2,1,0:T(8,128)} %raw_ref.7), custom_call_target="tpu_custom_call" | custom-call | flops 1000 | bytes 1000 | tf_op jit(solution)/shard_map/dress/pallas_call | solution.py:126
  17.6 0.6 collective-permute-start.2
  18.2 2.9 %collective-permute-start.3 = (f32[1032,128]{1,0:T(8,128)}, f32[1032,128]{1,0:T(8,128)S(1)}, u32[]{:S(2)}, u32[]{:S(2)}) collective-permute-start(f32[1032,128]{1,0:T(8,128)} %get-tuple-element.55), channel_id=1, source_target_pairs={{0,5},{1,6},{2,7},{3,4},{4,1},{5,2},{6,3},{7,0},{8,13},{9,14},{10,... | collective-permute-start | bytes 1585160 | tf_op jit(solution)/shard_map/ppermute | solution.py:499
  21.1 6.1 %dress.6 = (f32[1032,128]{1,0:T(8,128)}, f32[1032,128]{1,0:T(8,128)}) custom-call(s32[2]{0:T(128)} %pad_add_fusion.place_ref, f32[1,8,8,128,128]{4,3,2,1,0:T(8,128)} %left_ref.7, f32[1,8,8,128,128]{4,3,2,1,0:T(8,128)} %right_ref.7, f32[1,8,128,128]{3,2,1,0:T(8,128)} %raw_ref.7), custom_call_target="tpu_custom_call" | custom-call | flops 1000 | bytes 1000 | tf_op jit(solution)/shard_map/dress/pallas_call | solution.py:126
  27.2 0.0 copy-start.2
  27.2 1.1 %collective-permute-start.4 = (f32[1032,128]{1,0:T(8,128)}, f32[1032,128]{1,0:T(8,128)S(1)}, u32[]{:S(2)}, u32[]{:S(2)}) collective-permute-start(f32[1032,128]{1,0:T(8,128)} %get-tuple-element.58), channel_id=1, source_target_pairs={{0,3},{1,0},{2,1},{3,2},{4,11},{5,8},{6,9},{7,10},{8,7},{9,4},{10,... | collective-permute-start | bytes 1585160 | tf_op jit(solution)/shard_map/ppermute | solution.py:498
  28.3 6.1 %dress.7 = (f32[1032,128]{1,0:T(8,128)}, f32[1032,128]{1,0:T(8,128)}) custom-call(s32[2]{0:T(128)} %pad_add_fusion.place_ref, f32[1,8,8,128,128]{4,3,2,1,0:T(8,128)} %left_ref.7, f32[1,8,8,128,128]{4,3,2,1,0:T(8,128)} %right_ref.7, f32[1,8,128,128]{3,2,1,0:T(8,128)} %raw_ref.7), custom_call_target="tpu_custom_call" | custom-call | flops 1000 | bytes 1000 | tf_op jit(solution)/shard_map/dress/pallas_call | solution.py:126
  34.4 2.2 %collective-permute-start.5 = (f32[1032,128]{1,0:T(8,128)S(1)}, f32[1032,128]{1,0:T(8,128)S(1)}, u32[]{:S(2)}, u32[]{:S(2)}) collective-permute-start(f32[1032,128]{1,0:T(8,128)S(1)} %copy-done.3), channel_id=1, source_target_pairs={{0,7},{1,4},{2,5},{3,6},{4,3},{5,0},{6,1},{7,2},{8,15},{9,12},{10,... | collective-permute-start | bytes 1585160 | tf_op jit(solution)/shard_map/ppermute | solution.py:499
  36.5 10.5 %collective-permute-done.1.beta_ref = f32[1032,128]{1,0:T(8,128)S(1)} collective-permute-done((f32[1032,128]{1,0:T(8,128)}, f32[1032,128]{1,0:T(8,128)S(1)}, u32[]{:S(2)}, u32[]{:S(2)}) %collective-permute-start.1) | collective-permute-done | bytes 528416 | tf_op jit(solution)/shard_map/ppermute | solution.py:499
  47.1 2.3 %collective-permute-start.6 = (f32[1032,128]{1,0:T(8,128)}, f32[1032,128]{1,0:T(8,128)S(1)}, u32[]{:S(2)}, u32[]{:S(2)}) collective-permute-start(f32[1032,128]{1,0:T(8,128)} %get-tuple-element.62), channel_id=1, source_target_pairs={{0,0},{1,1},{2,2},{3,3},{4,8},{5,9},{6,10},{7,11},{8,4},{9,5},{10,... | collective-permute-start | bytes 1585160 | tf_op jit(solution)/shard_map/ppermute | solution.py:498
  49.4 1.4 %collective-permute-start.7 = (f32[1032,128]{1,0:T(8,128)}, f32[1032,128]{1,0:T(8,128)S(1)}, u32[]{:S(2)}, u32[]{:S(2)}) collective-permute-start(f32[1032,128]{1,0:T(8,128)} %get-tuple-element.63), channel_id=1, source_target_pairs={{0,4},{1,5},{2,6},{3,7},{4,0},{5,1},{6,2},{7,3},{8,12},{9,13},{10,... | collective-permute-start | bytes 1585160 | tf_op jit(solution)/shard_map/ppermute | solution.py:499
  50.8 2.5 %arrive.4 = (bf16[2048,256]{1,0:T(8,128)(2,1)S(1)}, bf16[2048,256]{1,0:T(8,128)(2,1)S(1)}, f32[2,128,128]{2,1,0:T(8,128)S(1)}) custom-call(s32[2]{0:T(128)S(1)} %copy-done.1, s32[1,2,8]{2,1,0:T(2,128)S(1)} %copy-done.2, f32[1,8,128,128]{3,2,1,0:T(8,128)S(1)} %copy-done, f32[2,128,128]{2,1,0:T(8,128)S(1)} %broadcast_in_dim.3.before_ref, ...), custom_call_target="tpu_custom_call" | custom-call | flops 1000 | bytes 1000 | tf_op jit(solution)/shard_map/arrive/pallas_call | solution.py:226
  53.4 5.0 %collective-permute-done.3.beta_ref = f32[1032,128]{1,0:T(8,128)S(1)} collective-permute-done((f32[1032,128]{1,0:T(8,128)}, f32[1032,128]{1,0:T(8,128)S(1)}, u32[]{:S(2)}, u32[]{:S(2)}) %collective-permute-start.3) | collective-permute-done | bytes 528416 | tf_op jit(solution)/shard_map/ppermute | solution.py:499
  58.3 2.5 %arrive.5 = (bf16[2048,256]{1,0:T(8,128)(2,1)S(1)}, bf16[2048,256]{1,0:T(8,128)(2,1)S(1)}, f32[2,128,128]{2,1,0:T(8,128)S(1)}) custom-call(s32[2]{0:T(128)S(1)} %copy-done.1, s32[1,2,8]{2,1,0:T(2,128)S(1)} %copy-done.2, f32[1,8,128,128]{3,2,1,0:T(8,128)S(1)} %copy-done, f32[2,128,128]{2,1,0:T(8,128)S(1)} %get-tuple-element.53.before_ref, ...), custom_call_target="tpu_custom_call" | custom-call | flops 1000 | bytes 1000 | tf_op jit(solution)/shard_map/arrive/pallas_call | solution.py:226
  60.9 2.5 %arrive.6 = (bf16[2048,256]{1,0:T(8,128)(2,1)S(1)}, bf16[2048,256]{1,0:T(8,128)(2,1)S(1)}, f32[2,128,128]{2,1,0:T(8,128)S(1)}) custom-call(s32[2]{0:T(128)S(1)} %copy-done.1, s32[1,2,8]{2,1,0:T(2,128)S(1)} %copy-done.2, f32[1,8,128,128]{3,2,1,0:T(8,128)S(1)} %copy-done, f32[2,128,128]{2,1,0:T(8,128)S(1)} %get-tuple-element.57.before_ref, ...), custom_call_target="tpu_custom_call" | custom-call | flops 1000 | bytes 1000 | tf_op jit(solution)/shard_map/arrive/pallas_call | solution.py:226
  63.4 2.5 %arrive.7 = (bf16[2048,256]{1,0:T(8,128)(2,1)S(1)}, bf16[2048,256]{1,0:T(8,128)(2,1)S(1)}, f32[2,128,128]{2,1,0:T(8,128)S(1)}) custom-call(s32[2]{0:T(128)S(1)} %copy-done.1, s32[1,2,8]{2,1,0:T(2,128)S(1)} %copy-done.2, f32[1,8,128,128]{3,2,1,0:T(8,128)S(1)} %copy-done, f32[2,128,128]{2,1,0:T(8,128)S(1)} %get-tuple-element.61.before_ref, ...), custom_call_target="tpu_custom_call" | custom-call | flops 1000 | bytes 1000 | tf_op jit(solution)/shard_map/arrive/pallas_call | solution.py:226
  65.9 14.6 %krylov.1 = (f32[6,2,128,128]{3,2,1,0:T(8,128)S(1)}, f32[8,128]{1,0:T(8,128)S(1)}) custom-call(s32[2]{0:T(128)S(1)} %copy-done.1, s32[1,2,8]{2,1,0:T(2,128)S(1)} %copy-done.2, f32[1,8,128,128]{3,2,1,0:T(8,128)S(1)} %copy-done, bf16[2048,256]{1,0:T(8,128)(2,1)S(1)} %get-tuple-element.52.refs_0_, bf16[2048,256]{1,0:T(8,128)(2,1)S(1)} %get-tuple-element.56.refs_1_, ...), custom_call_target="tpu_custom_call" | custom-call | flops 8589934592 | bytes 9437184 | tf_op jit(solution)/shard_map/krylov/pallas_call | solution.py:325
  80.4 10.1 %psum.7.report_ref = f32[8,128]{1,0:T(8,128)S(1)} all-reduce(f32[8,128]{1,0:T(8,128)S(1)} %get-tuple-element.70), channel_id=1, replica_groups=mesh['chain'=64,'term'=4] {'term'}, use_global_device_ids=true, to_apply=%region_0.0 | all-reduce | flops 1024 | bytes 8192 | tf_op jit(solution)/shard_map/psum | solution.py:505
  90.5 1.8 %davidson.1 = (f32[1,2,128,128]{3,2,1,0:T(8,128)}, f32[8,128]{1,0:T(8,128)S(1)}) custom-call(s32[2]{0:T(128)S(1)} %copy-done.1, f32[8,128]{1,0:T(8,128)S(1)} %psum.7.report_ref, f32[6,2,128,128]{3,2,1,0:T(8,128)S(1)} %get-tuple-element.71.basis_ref), custom_call_target="tpu_custom_call" | custom-call | tf_op jit(solution)/shard_map/davidson/pallas_call | solution.py:448
  92.3 0.5 slice.3
  (14 shorter events, 0.0 us)
Async XLA Ops:
  7.3 27.0 %collective-permute-start = (f32[1032,128]{1,0:T(8,128)}, f32[1032,128]{1,0:T(8,128)S(1)}, u32[]{:S(2)}, u32[]{:S(2)}) collective-permute-start(f32[1032,128]{1,0:T(8,128)} %get-tuple-element.50), channel_id=1, source_target_pairs={{0,2},{1,3},{2,0},{3,1},{4,10},{5,11},{6,8},{7,9},{8,6},{9,7},{10,... | collective-permute-start | bytes 1585160 | tf_op jit(solution)/shard_map/ppermute | solution.py:498
  10.0 37.1 %collective-permute-start.1 = (f32[1032,128]{1,0:T(8,128)}, f32[1032,128]{1,0:T(8,128)S(1)}, u32[]{:S(2)}, u32[]{:S(2)}) collective-permute-start(f32[1032,128]{1,0:T(8,128)} %get-tuple-element.51), channel_id=1, source_target_pairs={{0,6},{1,7},{2,4},{3,5},{4,2},{5,3},{6,0},{7,1},{8,14},{9,15},{10,... | collective-permute-start | bytes 1585160 | tf_op jit(solution)/shard_map/ppermute | solution.py:499
  17.6 31.8 %collective-permute-start.2 = (f32[1032,128]{1,0:T(8,128)}, f32[1032,128]{1,0:T(8,128)S(1)}, u32[]{:S(2)}, u32[]{:S(2)}) collective-permute-start(f32[1032,128]{1,0:T(8,128)} %get-tuple-element.54), channel_id=1, source_target_pairs={{0,1},{1,2},{2,3},{3,0},{4,9},{5,10},{6,11},{7,8},{8,5},{9,6},{10,... | collective-permute-start | bytes 1585160 | tf_op jit(solution)/shard_map/ppermute | solution.py:498
  18.2 40.1 %collective-permute-start.3 = (f32[1032,128]{1,0:T(8,128)}, f32[1032,128]{1,0:T(8,128)S(1)}, u32[]{:S(2)}, u32[]{:S(2)}) collective-permute-start(f32[1032,128]{1,0:T(8,128)} %get-tuple-element.55), channel_id=1, source_target_pairs={{0,5},{1,6},{2,7},{3,4},{4,1},{5,2},{6,3},{7,0},{8,13},{9,14},{10,... | collective-permute-start | bytes 1585160 | tf_op jit(solution)/shard_map/ppermute | solution.py:499
  27.2 7.2 %copy-start.3 = (f32[1032,128]{1,0:T(8,128)S(1)}, f32[1032,128]{1,0:T(8,128)}, u32[]{:S(2)}) copy-start(f32[1032,128]{1,0:T(8,128)} %get-tuple-element.59) | copy-start | bytes 1585156
  27.2 23.6 %copy-start = (f32[1,8,128,128]{3,2,1,0:T(8,128)S(1)}, f32[1,8,128,128]{3,2,1,0:T(8,128)}, u32[]{:S(2)}) copy-start(f32[1,8,128,128]{3,2,1,0:T(8,128)} %psi_ref.9) | copy-start | bytes 1572868
  27.2 23.7 %copy-start.1 = (s32[2]{0:T(128)S(1)}, s32[2]{0:T(128)}, u32[]{:S(2)}) copy-start(s32[2]{0:T(128)} %pad_add_fusion.place_ref) | copy-start | bytes 28
  27.2 23.7 %copy-start.2 = (s32[1,2,8]{2,1,0:T(2,128)S(1)}, s32[1,2,8]{2,1,0:T(2,128)}, u32[]{:S(2)}) copy-start(s32[1,2,8]{2,1,0:T(2,128)} %sizes_ref.9) | copy-start | bytes 196
  27.2 33.7 %collective-permute-start.4 = (f32[1032,128]{1,0:T(8,128)}, f32[1032,128]{1,0:T(8,128)S(1)}, u32[]{:S(2)}, u32[]{:S(2)}) collective-permute-start(f32[1032,128]{1,0:T(8,128)} %get-tuple-element.58), channel_id=1, source_target_pairs={{0,3},{1,0},{2,1},{3,2},{4,11},{5,8},{6,9},{7,10},{8,7},{9,4},{10,... | collective-permute-start | bytes 1585160 | tf_op jit(solution)/shard_map/ppermute | solution.py:498
  34.4 26.5 %collective-permute-start.5 = (f32[1032,128]{1,0:T(8,128)S(1)}, f32[1032,128]{1,0:T(8,128)S(1)}, u32[]{:S(2)}, u32[]{:S(2)}) collective-permute-start(f32[1032,128]{1,0:T(8,128)S(1)} %copy-done.3), channel_id=1, source_target_pairs={{0,7},{1,4},{2,5},{3,6},{4,3},{5,0},{6,1},{7,2},{8,15},{9,12},{10,... | collective-permute-start | bytes 1585160 | tf_op jit(solution)/shard_map/ppermute | solution.py:499
  47.1 16.3 %collective-permute-start.6 = (f32[1032,128]{1,0:T(8,128)}, f32[1032,128]{1,0:T(8,128)S(1)}, u32[]{:S(2)}, u32[]{:S(2)}) collective-permute-start(f32[1032,128]{1,0:T(8,128)} %get-tuple-element.62), channel_id=1, source_target_pairs={{0,0},{1,1},{2,2},{3,3},{4,8},{5,9},{6,10},{7,11},{8,4},{9,5},{10,... | collective-permute-start | bytes 1585160 | tf_op jit(solution)/shard_map/ppermute | solution.py:498
  49.4 14.0 %collective-permute-start.7 = (f32[1032,128]{1,0:T(8,128)}, f32[1032,128]{1,0:T(8,128)S(1)}, u32[]{:S(2)}, u32[]{:S(2)}) collective-permute-start(f32[1032,128]{1,0:T(8,128)} %get-tuple-element.63), channel_id=1, source_target_pairs={{0,4},{1,5},{2,6},{3,7},{4,0},{5,1},{6,2},{7,3},{8,12},{9,13},{10,... | collective-permute-start | bytes 1585160 | tf_op jit(solution)/shard_map/ppermute | solution.py:499

commit v3 on v2

v3 whole, which is shorter than its diff:
```python
import functools
import math

import jax
import jax.numpy as jnp
from jax import lax
from jax.experimental import pallas as pl
from jax.experimental.pallas import tpu as pltpu
from jax.sharding import PartitionSpec as P

ITERS = 4
NVEC = ITERS + 2
twist_scale = 0.22
shrink = 1.047
epsilon = 1e-06

B = 128
HALF = 64
F32 = jnp.float32
BF16 = jnp.bfloat16

OWNED = 2
LOCAL_TERMS = 8
MATS = OWNED * LOCAL_TERMS
DIAG_ROW = MATS * HALF
MSG_ROWS = DIAG_ROW + MATS // 2


def split(value):
    high = value.astype(BF16)
    low = (value - high.astype(F32)).astype(BF16)
    return high, low


def dot(left, right):
    return jnp.dot(left, right, preferred_element_type=F32)


def iotas(rows):
    row = lax.broadcasted_iota(jnp.int32, (rows, B), 0)
    lane = lax.broadcasted_iota(jnp.int32, (rows, B), 1)
    return row, lane


def swap_halves(value):
    return pltpu.roll(value, HALF, 1)


def dress_kernel(segments, groups, jobs, left_hbm, right_hbm, raw_hbm, *refs):
    outs, (env_ref, raw_ref, env_sem, raw_sem) = refs[: len(jobs)], refs[len(jobs) :]
    seg = lax.axis_index("chain")
    odd = lax.rem(seg, 2) == 1
    edge = jnp.logical_or(seg == 0, seg == segments - 1)

    def first_sector(slot):
        return OWNED * lax.rem(lax.axis_index("term") + jobs[slot][1], groups)

    def env_copy(source, slot, owned):
        part = source.at[0, :, first_sector(slot) + owned]
        return pltpu.make_async_copy(part, env_ref.at[slot, owned], env_sem.at[slot, owned])

    def raw_copy(slot):
        part = raw_hbm.at[0, pl.ds(first_sector(slot), OWNED)]
        return pltpu.make_async_copy(part, raw_ref.at[slot], raw_sem.at[slot])

    for slot, (side, _) in enumerate(jobs):
        raw_copy(slot).start()
        take_left = jnp.logical_not(odd) if side else jnp.logical_xor(odd, edge)

        @pl.when(take_left)
        def _():
            for owned in range(OWNED):
                env_copy(left_hbm, slot, owned).start()

        @pl.when(jnp.logical_not(take_left))
        def _():
            for owned in range(OWNED):
                env_copy(right_hbm, slot, owned).start()

    row, lane = iotas(B)
    eye = jnp.where(row == lane, 1.0, 0.0).astype(F32)
    sign = jnp.where(odd, 1.0, -1.0).astype(F32)
    row_h, lane_h = iotas(HALF)
    keep_top = jnp.logical_or(lane_h >= HALF, lane_h >= row_h)
    on_diag_high = lane_h - HALF == row_h
    on_diag_low = lane_h == row_h
    pairs = LOCAL_TERMS // 2
    for slot, (side, _) in enumerate(jobs):
        raw_copy(slot).wait()
        out_ref = outs[slot]
        if side:
            even, coef = eye * (1.0 / shrink), -sign
        else:
            even = eye * jnp.where(edge, 1.0, 1.0 / shrink).astype(F32)
            coef = jnp.where(edge, 0.0, sign).astype(F32)
        coef = coef * (twist_scale / math.sqrt(2.0 * B) / shrink)
        factors = []
        for owned in range(OWNED):
            raw = raw_ref[slot, owned]
            odd_part = (raw - raw.T) * coef
            high, low = split((even + odd_part) * 0.5)
            right_op = jnp.concatenate([jnp.concatenate([high, low], 1)] * 2, 0)
            high, low = split(even - odd_part)
            left_op = jnp.concatenate([jnp.concatenate([high] * 2, 1), jnp.concatenate([low] * 2, 1)], 0)
            factors.append((left_op, right_op))
        for owned in range(OWNED):
            env_copy(left_hbm, slot, owned).wait()
        work = [(owned, pair) for owned in range(OWNED) for pair in range(pairs)]
        parts = []
        for owned, pair in work:
            sums = []
            for term in (2 * pair, 2 * pair + 1):
                env = env_ref[slot, owned, term]
                high, low = split(env + env.T)
                sums.append(jnp.concatenate([high, low], 1))
            parts.append(dot(jnp.concatenate(sums, 0), factors[owned][1]))
        fulls = []
        for (owned, pair), part in zip(work, parts):
            high, low = split(part[:, :B] + part[:, B:])
            right_side = jnp.concatenate(
                [jnp.concatenate([high[:B], high[B:]], 1), jnp.concatenate([low[:B], low[B:]], 1)], 0
            )
            full = dot(factors[owned][0], right_side)
            fulls.append(full[:B] + full[B:])
        for index, full in enumerate(fulls):
            diag = jnp.zeros((HALF, B), F32)
            for j in range(2):
                mat = full[:, j * B : (j + 1) * B]
                top, bottom = mat[:HALF], mat[HALF:]
                turned = swap_halves(bottom)
                start = (2 * index + j) * HALF
                out_ref[start : start + HALF, :] = jnp.where(keep_top, top, turned)
                if j == 0:
                    diag = jnp.where(on_diag_high, bottom, diag)
                else:
                    diag = jnp.where(on_diag_low, turned, diag)
            start = DIAG_ROW + index
            out_ref[start : start + 1, :] = jnp.sum(diag, axis=0, keepdims=True)


TINY = pl.CostEstimate(flops=1000, bytes_accessed=1000, transcendentals=0)
VMEM = pl.BlockSpec(memory_space=pltpu.VMEM)
SMEM = pl.BlockSpec(memory_space=pltpu.SMEM)
BLOCK_ROWS = MATS * B


def dress(left_env, right_env, raw, jobs, segments, groups, limit):
    count = len(jobs)
    return pl.pallas_call(
        functools.partial(dress_kernel, segments, groups, jobs),
        out_shape=(jax.ShapeDtypeStruct((MSG_ROWS, B), F32),) * count,
        in_specs=[pl.BlockSpec(memory_space=pltpu.HBM)] * 3,
        out_specs=(VMEM,) * count,
        scratch_shapes=[
            pltpu.VMEM((count, OWNED, LOCAL_TERMS, B, B), F32),
            pltpu.VMEM((count, OWNED, B, B), F32),
            pltpu.SemaphoreType.DMA((count, OWNED)),
            pltpu.SemaphoreType.DMA((count,)),
        ],
        compiler_params=pltpu.CompilerParams(vmem_limit_bytes=limit << 20),
        cost_estimate=TINY,
        name="dress",
    )(left_env, right_env, raw)


def total(value):
    tiles = jnp.sum(value.reshape(OWNED * B // 8, 8, B), axis=0)
    return jnp.sum(jnp.sum(tiles, axis=0, keepdims=True), axis=1, keepdims=True)


def unpack(msg_ref, pairs):
    row_h, lane_h = iotas(HALF)
    keep_top = jnp.logical_or(lane_h >= HALF, lane_h >= row_h)
    keep_bottom = jnp.logical_and(lane_h >= HALF, lane_h - HALF < row_h)
    on_diag = lane_h - HALF == row_h
    packed = [msg_ref[2 * pair * HALF : (2 * pair + 2) * HALF, :] for pair in pairs]
    diags = [msg_ref[DIAG_ROW + pair : DIAG_ROW + pair + 1, :] for pair in pairs]
    out = []
    for pair_value, diag_row in zip(packed, diags):
        for j in range(2):
            value = pair_value[j * HALF : (j + 1) * HALF]
            turned = swap_halves(value)
            flipped = jnp.concatenate([value, turned], 0).T
            diag = diag_row if j == 0 else swap_halves(diag_row)
            top = jnp.where(keep_top, value, flipped[:HALF])
            bottom = jnp.where(keep_bottom, turned, flipped[HALF:])
            bottom = jnp.where(on_diag, jnp.broadcast_to(diag, (HALF, B)), bottom)
            high, low = split(jnp.concatenate([top, bottom], 0))
            out.append(jnp.concatenate([high, low], 1))
    return out


def doubled(vector):
    high, low = split(vector)
    return jnp.concatenate([jnp.concatenate([high, low], 1)] * 2, 0)


def between(half):
    high, low = split(half[:, :B] + half[:, B:])
    return jnp.concatenate(
        [jnp.concatenate([high[:B], high[B:]], 1), jnp.concatenate([low[:B], low[B:]], 1)], 0
    )


def quarters(out):
    return (out[:B, :B] + out[:B, B:]) + (out[B:, :B] + out[B:, B:])


def live_mask(sizes_ref, owned):
    odd = lax.rem(lax.axis_index("chain"), 2) == 1
    sector = OWNED * lax.axis_index("term") + owned
    row, lane = iotas(B)
    rows_live = sizes_ref[0, 0, sector]
    cols_live = sizes_ref[0, 1, sector]
    first = jnp.where(odd, cols_live, rows_live)
    second = jnp.where(odd, rows_live, cols_live)
    return jnp.where(jnp.logical_and(row < first, lane < second), 1.0, 0.0).astype(F32)


def start_vector(sizes_ref, psi_ref, owned):
    odd = lax.rem(lax.axis_index("chain"), 2) == 1
    guess = psi_ref[0, OWNED * lax.axis_index("term") + owned]
    return jnp.where(odd, guess.T, guess) * live_mask(sizes_ref, owned)


def arrive_kernel(sizes_ref, psi_ref, before_ref, alpha_ref, beta_ref, left_ref, right_ref, image_ref):
    pairs = LOCAL_TERMS // 2
    for owned in range(OWNED):
        vector = doubled(start_vector(sizes_ref, psi_ref, owned))
        which = [owned * pairs + i for i in range(pairs)]
        rows = slice(owned * LOCAL_TERMS * B, (owned + 1) * LOCAL_TERMS * B)
        lefts = unpack(alpha_ref, which)
        left_ref[rows, :] = jnp.concatenate(lefts, 0)
        mids = [between(dot(jnp.concatenate(lefts[2 * i : 2 * i + 2], 0), vector)) for i in range(pairs)]
        rights = jnp.concatenate(unpack(beta_ref, which), 0)
        right_ref[rows, :] = rights
        image_ref[owned] = before_ref[owned] + quarters(dot(jnp.concatenate(mids, 1), rights))


def arrive(sizes, psi, before, alpha, beta):
    block = jax.ShapeDtypeStruct((BLOCK_ROWS, 2 * B), BF16)
    return pl.pallas_call(
        arrive_kernel,
        out_shape=(block, block, jax.ShapeDtypeStruct((OWNED, B, B), F32)),
        in_specs=[SMEM] + [VMEM] * 4,
        out_specs=(VMEM,) * 3,
        compiler_params=pltpu.CompilerParams(vmem_limit_bytes=16 << 20),
        cost_estimate=TINY,
        name="arrive",
    )(sizes, psi, before, alpha, beta)


def krylov_kernel(sizes_ref, psi_ref, *refs):
    lefts, rights, image_ref = refs[0:4], refs[4:8], refs[8]
    basis_ref, report_ref = refs[9:11]
    vec_ref, acc_ref, mask_ref = refs[11:]
    group = lax.axis_index("term")
    starts = []
    for owned in range(OWNED):
        mask_ref[owned] = live_mask(sizes_ref, owned)
        starts.append(start_vector(sizes_ref, psi_ref, owned))
    vector = jnp.stack(starts, 0)

    def apply_ham():
        acc_ref[...] = jnp.zeros_like(acc_ref)

        def body(index, carry):
            units = []
            for owned in range(OWNED):
                start = pl.multiple_of((owned * (LOCAL_TERMS // 2) + index) * 2 * B, 2 * B)
                units.append([between(dot(left[pl.ds(start, 2 * B), :], vec_ref[owned])) for left in lefts])
            for owned in range(OWNED):
                start = pl.multiple_of((owned * (LOCAL_TERMS // 2) + index) * 2 * B, 2 * B)
                right = jnp.concatenate([ref[pl.ds(start, 2 * B), :] for ref in rights], 0)
                acc_ref[owned] += quarters(dot(jnp.concatenate(units[owned], 1), right))
            return carry

        lax.fori_loop(0, LOCAL_TERMS // 2, body, 0, unroll=True)
        return acc_ref[...] * mask_ref[...]

    def inverse_norm(square):
        return jnp.where(square > 0.0, lax.rsqrt(jnp.where(square > 0.0, square, 1.0)), 0.0)

    lane_1 = lax.broadcasted_iota(jnp.int32, (1, B), 1)
    report = jnp.zeros((1, B), F32)

    def put(report, slot, value):
        return jnp.where(lane_1 == slot, value, report)

    grams = []

    def partial_dot(first, second):
        return jnp.sum((first * second).reshape(OWNED * B, B), axis=0, keepdims=True)

    square = total(vector * vector)
    scale = inverse_norm(square)
    report = put(report, 0, square * scale)
    basis_ref[0] = vector * scale
    previous_beta = None
    for step in range(NVEC - 1):
        current = basis_ref[step]
        if step:
            for owned in range(OWNED):
                vec_ref[owned] = doubled(current[owned])
            image = apply_ham()
        else:
            image = image_ref[...] * mask_ref[...] * scale
        alpha = total(current * image)
        rest = image - alpha * current
        if step:
            rest = rest - previous_beta * basis_ref[step - 1]
        square = total(rest * rest)
        scale = inverse_norm(square)
        beta = square * scale
        basis_ref[step + 1] = rest * scale
        grams += [partial_dot(basis_ref[step], basis_ref[i]) for i in range(step + 1)]
        report = put(report, 1 + step, alpha)
        report = put(report, 1 + (NVEC - 1) + step, beta)
        previous_beta = beta
    grams += [partial_dot(basis_ref[NVEC - 1], basis_ref[i]) for i in range(NVEC)]
    first = 1 + 2 * (NVEC - 1)
    rows = [jnp.zeros((1, B), F32)] * first + grams
    rows += [jnp.zeros((1, B), F32)] * (B - len(rows))
    summed = jnp.sum(jnp.concatenate(rows, 0).T, axis=0, keepdims=True)
    report = report + summed
    row_8, _ = iotas(8)
    report_ref[...] = jnp.where(row_8 == group, jnp.broadcast_to(report, (8, B)), 0.0)


def krylov(sizes, psi, lefts, rights, image):
    return pl.pallas_call(
        krylov_kernel,
        out_shape=(
            jax.ShapeDtypeStruct((NVEC, OWNED, B, B), F32),
            jax.ShapeDtypeStruct((8, B), F32),
        ),
        in_specs=[SMEM] + [VMEM] * 10,
        out_specs=(VMEM, VMEM),
        scratch_shapes=[
            pltpu.VMEM((OWNED, 2 * B, 2 * B), BF16),
            pltpu.VMEM((OWNED, B, B), F32),
            pltpu.VMEM((OWNED, B, B), F32),
        ],
        compiler_params=pltpu.CompilerParams(vmem_limit_bytes=24 << 20),
        cost_estimate=TINY,
        name="krylov",
    )(sizes, psi, *lefts, *rights, image)


def davidson_kernel(volume, report_ref, basis_ref, out_ref, energy_ref):
    odd = lax.rem(lax.axis_index("chain"), 2) == 1
    group = lax.axis_index("term")
    report = report_ref[...]
    row_8, lane_8 = iotas(8)

    def column(slot):
        return jnp.sum(jnp.where(lane_8 == slot, report, 0.0), axis=1, keepdims=True)

    weight = column(0)
    alphas = [column(1 + i) for i in range(NVEC - 1)]
    betas = [column(NVEC + i) for i in range(NVEC - 1)]
    gram = {}
    slot = 1 + 2 * (NVEC - 1)
    for j in range(NVEC):
        for i in range(j + 1):
            gram[i, j] = gram[j, i] = column(slot)
            slot += 1

    def mean_dot(first, second):
        parts = None
        for i, a in enumerate(first):
            inner = None
            for j, b in enumerate(second):
                piece = gram[i, j] * b
                inner = piece if inner is None else inner + piece
            piece = a * inner
            parts = piece if parts is None else parts + piece
        return jnp.sum(parts, axis=0, keepdims=True) / volume

    def apply_ham(vector):
        size = len(vector)
        out = []
        for i in range(size + 1):
            value = jnp.zeros((8, 1), F32)
            if i < size:
                value = value + alphas[i] * vector[i]
            if i >= 1:
                value = value + betas[i - 1] * vector[i - 1]
            if i + 1 < size:
                value = value + betas[i] * vector[i + 1]
            out.append(value)
        return out

    def combine(a, first, b, second):
        out = []
        for i in range(max(len(first), len(second))):
            value = None
            if i < len(first):
                value = a * first[i]
            if i < len(second):
                piece = b * second[i]
                value = piece if value is None else value + piece
            out.append(value)
        return out

    started = [weight]
    norm = jnp.sqrt(mean_dot(started, started) + epsilon)
    vector = [weight / norm]
    image = apply_ham(vector)
    energy = mean_dot(vector, image)
    for _ in range(ITERS):
        residual = combine(1.0, image, -energy, vector)
        norm = jnp.sqrt(mean_dot(residual, residual) + epsilon)
        along = mean_dot(residual, image) / norm
        unit = [value / norm for value in residual]
        image_unit = apply_ham(unit)
        curve = mean_dot(unit, image_unit)
        gap_half = 0.5 * (curve - energy)
        lowest = 0.5 * (curve + energy) - jnp.sqrt(gap_half * gap_half + along * along)
        coef_b = lowest - energy
        combined = jnp.sqrt(along * along + coef_b * coef_b)
        vector = combine(along / combined, vector, coef_b / combined, unit)
        image = combine(along / combined, image, coef_b / combined, image_unit)
        energy = lowest

    mine = lax.broadcasted_iota(jnp.int32, (8, 1), 0) == group
    coefs = [jnp.sum(jnp.where(mine, value, 0.0), axis=0, keepdims=True) for value in vector]
    for owned in range(OWNED):
        value = None
        for i, coef in enumerate(coefs):
            piece = coef * basis_ref[i, owned]
            value = piece if value is None else value + piece
        out_ref[0, owned] = jnp.where(odd, value.T, value)
    energy_ref[0] = energy[0, 0]


def davidson(report, basis, volume):
    return pl.pallas_call(
        functools.partial(davidson_kernel, volume),
        out_shape=(
            jax.ShapeDtypeStruct((1, OWNED, B, B), F32),
            jax.ShapeDtypeStruct((1,), F32),
        ),
        in_specs=[VMEM, VMEM],
        out_specs=(VMEM, SMEM),
        compiler_params=pltpu.CompilerParams(vmem_limit_bytes=16 << 20),
        cost_estimate=TINY,
        name="davidson",
    )(report, basis)


ORDER = (
    (((0, 2), (1, 2)), 20),
    (((0, 1), (1, 1)), 20),
    (((0, 3), (1, 3)), 20),
    (((0, 0), (1, 0)), 20),
)


def exchange_pairs(segments, groups, partner, offset):
    return [
        (seg * groups + term, partner(seg) * groups + (term + offset) % groups)
        for seg in range(segments)
        for term in range(groups)
    ]


def local(segments, groups, psi_guess, transfer_raw, left_env, right_env, block_sizes):
    def alpha_partner(seg):
        if seg in (0, segments - 1):
            return seg
        return seg + 1 if seg % 2 else seg - 1

    def beta_partner(seg):
        return seg ^ 1

    partners = (alpha_partner, beta_partner)
    left_env, right_env, raw = [
        pltpu.with_memory_space_constraint(value, pltpu.HBM) for value in (left_env, right_env, transfer_raw)
    ]
    messages = {}
    for jobs, limit in ORDER:
        made = dress(left_env, right_env, raw, jobs, segments, groups, limit)
        made, raw = lax.optimization_barrier((made, raw))
        for job, message in zip(jobs, made):
            messages[job] = message

    def send(side, offset, after=None):
        message = messages[side, offset]
        if after is not None:
            message, _ = lax.optimization_barrier((message, after))
        return lax.ppermute(message, ("chain", "term"), exchange_pairs(segments, groups, partners[side], offset))

    alphas, betas = {}, {}
    for offset in (2, 1, 3, 0):
        alphas[offset] = send(0, offset)
        betas[offset] = send(1, offset)
    lefts, rights = [], []
    image = jnp.zeros((OWNED, B, B), F32)
    for offset in (2, 1, 3, 0):
        left, right, image = arrive(block_sizes, psi_guess, image, alphas[offset], betas[offset])
        lefts.append(left)
        rights.append(right)
    volume = float(psi_guess.shape[1] * B * B)
    basis, report = krylov(block_sizes, psi_guess, lefts, rights, image)
    report = lax.psum(report, "term")
    vector, energy = davidson(report, basis, volume)
    return vector, energy


def solution(mesh):
    segments, groups = mesh.shape["chain"], mesh.shape["term"]
    placed = (
        P("chain", None, None, None),
        P("chain", None, None, None),
        P("chain", "term", None, None, None),
        P("chain", "term", None, None, None),
        P("chain", None, None),
    )
    return jax.shard_map(
        functools.partial(local, segments, groups),
        mesh=mesh,
        in_specs=placed,
        out_specs=(P("chain", "term", None, None), P("chain")),
        check_vma=False,
    )
```

time: 93.2 us -> 84.8 us (0.910)
  Pallas kernels: 50.6 us -> 35.4 us
  waiting for transfers between devices: 15.5 us -> 23.3 us
    pallas_call x8, Pallas kernels: 34.3 us -> 22.2 us  [the longest x4 14.3 us: dress(): pl.pallas_call(functools.partial(dress_kernel, segments, groups, jobs), o...]
    ppermute x8, waiting for transfers between devices: 15.5 us -> 23.3 us  [send(): lax.ppermute(message, ('chain', 'term'), exchange_pairs(segments, groups,...]
    pallas_call x1, Pallas kernels: 14.6 us -> 12 us  [krylov(): pl.pallas_call(krylov_kernel, out_shape=(jax.ShapeDtypeStruct((NVEC, OWNE...]
  transfers between devices with their start and end apart: 8 -> 8, of which waited for: 2 -> 2; matrix products, arithmetic and copies ran while one was open for 0% -> 0% of each run, Pallas kernels for 28% -> 20%
where the time goes in v3:
time: 84.8 us; the launch traced here: 83.9 us
  Pallas kernels  35.4 us (42%)
  waiting for transfers between devices  23.3 us (27%)
  starting transfers between devices  14.5 us (17%)
  blocking collectives  9.57 us (11%)
  between operations  0.97 us (1%)
    ppermute x8, waiting for transfers between devices, send(): lax.ppermute(message, ('chain', 'term'), exchange_pairs(segments, groups,...  23.3 us
    ppermute x8, starting transfers between devices, send(): lax.ppermute(message, ('chain', 'term'), exchange_pairs(segments, groups,...  14.5 us
    pallas_call x4, Pallas kernels, dress(): pl.pallas_call(functools.partial(dress_kernel, segments, groups, jobs), o...  14.3 us
    pallas_call x1, Pallas kernels, krylov(): pl.pallas_call(krylov_kernel, out_shape=(jax.ShapeDtypeStruct((NVEC, OWNE...  12 us
    psum x1, blocking collectives, local(): report = lax.psum(report, 'term')  9.57 us
    pallas_call x4, Pallas kernels, arrive(): pl.pallas_call(arrive_kernel, out_shape=(block, block, jax.ShapeDtypeStru...  7.92 us
  transfers between devices with their start and end apart: 8, of which 2 were waited for; matrix products, arithmetic and copies ran while one was open for 0% of the time, Pallas kernels for 20%

profile of v3, /device:TPU:2, one launch (start us, length us, event | category | flops | bytes accessed | tf_op | source)
XLA Modules:
  0.0 83.9 jit_solution(12755818170769697331)
XLA Ops:
  0.6 3.6 %dress.4 = (f32[1032,128]{1,0:T(8,128)S(1)}, f32[1032,128]{1,0:T(8,128)S(1)}) custom-call(f32[1,8,8,128,128]{4,3,2,1,0:T(8,128)} %left_hbm.7, f32[1,8,8,128,128]{4,3,2,1,0:T(8,128)} %right_hbm.7, f32[1,8,128,128]{3,2,1,0:T(8,128)} %raw_hbm.4), custom_call_target="tpu_custom_call" | custom-call | flops 1000 | bytes 1000 | tf_op jit(solution)/shard_map/dress/pallas_call | solution.py:149
  4.2 2.4 %collective-permute-start = (f32[1032,128]{1,0:T(8,128)S(1)}, f32[1032,128]{1,0:T(8,128)S(1)}, u32[]{:S(2)}, u32[]{:S(2)}) collective-permute-start(f32[1032,128]{1,0:T(8,128)S(1)} %get-tuple-element.37), channel_id=1, source_target_pairs={{0,2},{1,3},{2,0},{3,1},{4,10},{5,11},{6,8},{7,9},{8,6},{9,7},{10,... | collective-permute-start | bytes 1585160 | tf_op jit(solution)/shard_map/ppermute | solution.py:492
  6.6 1.9 %collective-permute-start.1 = (f32[1032,128]{1,0:T(8,128)S(1)}, f32[1032,128]{1,0:T(8,128)S(1)}, u32[]{:S(2)}, u32[]{:S(2)}) collective-permute-start(f32[1032,128]{1,0:T(8,128)S(1)} %get-tuple-element.38), channel_id=1, source_target_pairs={{0,6},{1,7},{2,4},{3,5},{4,2},{5,3},{6,0},{7,1},{8,14},{9,15},{10,... | collective-permute-start | bytes 1585160 | tf_op jit(solution)/shard_map/ppermute | solution.py:492
  8.5 3.6 %dress.5 = (f32[1032,128]{1,0:T(8,128)S(1)}, f32[1032,128]{1,0:T(8,128)S(1)}) custom-call(f32[1,8,8,128,128]{4,3,2,1,0:T(8,128)} %left_hbm.7, f32[1,8,8,128,128]{4,3,2,1,0:T(8,128)} %right_hbm.7, f32[1,8,128,128]{3,2,1,0:T(8,128)} %raw_hbm.4), custom_call_target="tpu_custom_call" | custom-call | flops 1000 | bytes 1000 | tf_op jit(solution)/shard_map/dress/pallas_call | solution.py:149
  12.1 0.5 collective-permute-start.2
  12.6 3.1 %collective-permute-start.3 = (f32[1032,128]{1,0:T(8,128)S(1)}, f32[1032,128]{1,0:T(8,128)S(1)}, u32[]{:S(2)}, u32[]{:S(2)}) collective-permute-start(f32[1032,128]{1,0:T(8,128)S(1)} %get-tuple-element.45), channel_id=1, source_target_pairs={{0,5},{1,6},{2,7},{3,4},{4,1},{5,2},{6,3},{7,0},{8,13},{9,14},{10,... | collective-permute-start | bytes 1585160 | tf_op jit(solution)/shard_map/ppermute | solution.py:492
  15.6 3.6 %dress.6 = (f32[1032,128]{1,0:T(8,128)S(1)}, f32[1032,128]{1,0:T(8,128)S(1)}) custom-call(f32[1,8,8,128,128]{4,3,2,1,0:T(8,128)} %left_hbm.7, f32[1,8,8,128,128]{4,3,2,1,0:T(8,128)} %right_hbm.7, f32[1,8,128,128]{3,2,1,0:T(8,128)} %raw_hbm.4), custom_call_target="tpu_custom_call" | custom-call | flops 1000 | bytes 1000 | tf_op jit(solution)/shard_map/dress/pallas_call | solution.py:149
  19.2 0.0 copy-start
  19.2 0.0 copy-start.1
  19.2 0.8 collective-permute-start.4
  20.1 3.6 %dress.7 = (f32[1032,128]{1,0:T(8,128)S(1)}, f32[1032,128]{1,0:T(8,128)S(1)}) custom-call(f32[1,8,8,128,128]{4,3,2,1,0:T(8,128)} %left_hbm.7, f32[1,8,8,128,128]{4,3,2,1,0:T(8,128)} %right_hbm.7, f32[1,8,128,128]{3,2,1,0:T(8,128)} %raw_hbm.4), custom_call_target="tpu_custom_call" | custom-call | flops 1000 | bytes 1000 | tf_op jit(solution)/shard_map/dress/pallas_call | solution.py:149
  23.7 2.1 %collective-permute-start.5 = (f32[1032,128]{1,0:T(8,128)S(1)}, f32[1032,128]{1,0:T(8,128)S(1)}, u32[]{:S(2)}, u32[]{:S(2)}) collective-permute-start(f32[1032,128]{1,0:T(8,128)S(1)} %get-tuple-element.52), channel_id=1, source_target_pairs={{0,7},{1,4},{2,5},{3,6},{4,3},{5,0},{6,1},{7,2},{8,15},{9,12},{10,... | collective-permute-start | bytes 1585160 | tf_op jit(solution)/shard_map/ppermute | solution.py:492
  25.8 17.9 %collective-permute-done.1.beta_ref = f32[1032,128]{1,0:T(8,128)S(1)} collective-permute-done((f32[1032,128]{1,0:T(8,128)S(1)}, f32[1032,128]{1,0:T(8,128)S(1)}, u32[]{:S(2)}, u32[]{:S(2)}) %collective-permute-start.1) | collective-permute-done | bytes 528416 | tf_op jit(solution)/shard_map/ppermute | solution.py:492
  43.7 2.4 %collective-permute-start.6 = (f32[1032,128]{1,0:T(8,128)S(1)}, f32[1032,128]{1,0:T(8,128)S(1)}, u32[]{:S(2)}, u32[]{:S(2)}) collective-permute-start(f32[1032,128]{1,0:T(8,128)S(1)} %get-tuple-element.58), channel_id=1, source_target_pairs={{0,0},{1,1},{2,2},{3,3},{4,8},{5,9},{6,10},{7,11},{8,4},{9,5},{10,... | collective-permute-start | bytes 1585160 | tf_op jit(solution)/shard_map/ppermute | solution.py:492
  46.1 0.0 collective-permute-done.2.alpha_ref
  46.1 1.4 %collective-permute-start.7 = (f32[1032,128]{1,0:T(8,128)S(1)}, f32[1032,128]{1,0:T(8,128)S(1)}, u32[]{:S(2)}, u32[]{:S(2)}) collective-permute-start(f32[1032,128]{1,0:T(8,128)S(1)} %get-tuple-element.59), channel_id=1, source_target_pairs={{0,4},{1,5},{2,6},{3,7},{4,0},{5,1},{6,2},{7,3},{8,12},{9,13},{10,... | collective-permute-start | bytes 1585160 | tf_op jit(solution)/shard_map/ppermute | solution.py:492
  47.5 2.0 %arrive.4 = (bf16[2048,256]{1,0:T(8,128)(2,1)S(1)}, bf16[2048,256]{1,0:T(8,128)(2,1)S(1)}, f32[2,128,128]{2,1,0:T(8,128)S(1)}) custom-call(s32[1,2,8]{2,1,0:T(2,128)S(1)} %copy-done.1, f32[1,8,128,128]{3,2,1,0:T(8,128)S(1)} %copy-done, f32[2,128,128]{2,1,0:T(8,128)S(1)} %broadcast_in_dim.3.before_ref, f32[1032,128]{1,0:T(8,128)S(1)} %collective-permute-done.alpha_ref, ...), custom_call_target="tpu_custom_call" | custom-call | flops 1000 | bytes 1000 | tf_op jit(solution)/shard_map/arrive/pallas_call | solution.py:242
  49.5 5.4 %collective-permute-done.3.beta_ref = f32[1032,128]{1,0:T(8,128)S(1)} collective-permute-done((f32[1032,128]{1,0:T(8,128)S(1)}, f32[1032,128]{1,0:T(8,128)S(1)}, u32[]{:S(2)}, u32[]{:S(2)}) %collective-permute-start.3) | collective-permute-done | bytes 528416 | tf_op jit(solution)/shard_map/ppermute | solution.py:492
  54.9 2.0 %arrive.5 = (bf16[2048,256]{1,0:T(8,128)(2,1)S(1)}, bf16[2048,256]{1,0:T(8,128)(2,1)S(1)}, f32[2,128,128]{2,1,0:T(8,128)S(1)}) custom-call(s32[1,2,8]{2,1,0:T(2,128)S(1)} %copy-done.1, f32[1,8,128,128]{3,2,1,0:T(8,128)S(1)} %copy-done, f32[2,128,128]{2,1,0:T(8,128)S(1)} %get-tuple-element.40.before_ref, f32[1032,128]{1,0:T(8,128)S(1)} %collective-permute-done.2.alpha_ref, ...), custom_call_target="tpu_custom_call" | custom-call | flops 1000 | bytes 1000 | tf_op jit(solution)/shard_map/arrive/pallas_call | solution.py:242
  56.9 2.0 %arrive.6 = (bf16[2048,256]{1,0:T(8,128)(2,1)S(1)}, bf16[2048,256]{1,0:T(8,128)(2,1)S(1)}, f32[2,128,128]{2,1,0:T(8,128)S(1)}) custom-call(s32[1,2,8]{2,1,0:T(2,128)S(1)} %copy-done.1, f32[1,8,128,128]{3,2,1,0:T(8,128)S(1)} %copy-done, f32[2,128,128]{2,1,0:T(8,128)S(1)} %get-tuple-element.47.before_ref, f32[1032,128]{1,0:T(8,128)S(1)} %collective-permute-done.4.alpha_ref, ...), custom_call_target="tpu_custom_call" | custom-call | flops 1000 | bytes 1000 | tf_op jit(solution)/shard_map/arrive/pallas_call | solution.py:242
  58.9 2.0 %arrive.7 = (bf16[2048,256]{1,0:T(8,128)(2,1)S(1)}, bf16[2048,256]{1,0:T(8,128)(2,1)S(1)}, f32[2,128,128]{2,1,0:T(8,128)S(1)}) custom-call(s32[1,2,8]{2,1,0:T(2,128)S(1)} %copy-done.1, f32[1,8,128,128]{3,2,1,0:T(8,128)S(1)} %copy-done, f32[2,128,128]{2,1,0:T(8,128)S(1)} %get-tuple-element.54.before_ref, f32[1032,128]{1,0:T(8,128)S(1)} %collective-permute-done.6.alpha_ref, ...), custom_call_target="tpu_custom_call" | custom-call | flops 1000 | bytes 1000 | tf_op jit(solution)/shard_map/arrive/pallas_call | solution.py:242
  60.9 12.0 %krylov.1 = (f32[6,2,128,128]{3,2,1,0:T(8,128)S(1)}, f32[8,128]{1,0:T(8,128)S(1)}) custom-call(s32[1,2,8]{2,1,0:T(2,128)S(1)} %copy-done.1, f32[1,8,128,128]{3,2,1,0:T(8,128)S(1)} %copy-done, bf16[2048,256]{1,0:T(8,128)(2,1)S(1)} %get-tuple-element.39.refs_0_, bf16[2048,256]{1,0:T(8,128)(2,1)S(1)} %get-tuple-element.46.refs_1_, ...), custom_call_target="tpu_custom_call" | custom-call | flops 1000 | bytes 1000 | tf_op jit(solution)/shard_map/krylov/pallas_call | solution.py:331
  72.9 9.6 %psum.7.report_ref = f32[8,128]{1,0:T(8,128)S(1)} all-reduce(f32[8,128]{1,0:T(8,128)S(1)} %get-tuple-element.66), channel_id=1, replica_groups=mesh['chain'=64,'term'=4] {'term'}, use_global_device_ids=true, to_apply=%region_0.0 | all-reduce | flops 1024 | bytes 8192 | tf_op jit(solution)/shard_map/psum | solution.py:506
  82.4 1.2 %davidson.1 = (f32[1,2,128,128]{3,2,1,0:T(8,128)}, f32[1]{0:T(128)}) custom-call(f32[8,128]{1,0:T(8,128)S(1)} %psum.7.report_ref, f32[6,2,128,128]{3,2,1,0:T(8,128)S(1)} %get-tuple-element.67.basis_ref), custom_call_target="tpu_custom_call" | custom-call | flops 1000 | bytes 1000 | tf_op jit(solution)/shard_map/davidson/pallas_call | solution.py:438
  (8 shorter events, 0.0 us)
Async XLA Ops:
  4.2 19.4 %collective-permute-start = (f32[1032,128]{1,0:T(8,128)S(1)}, f32[1032,128]{1,0:T(8,128)S(1)}, u32[]{:S(2)}, u32[]{:S(2)}) collective-permute-start(f32[1032,128]{1,0:T(8,128)S(1)} %get-tuple-element.37), channel_id=1, source_target_pairs={{0,2},{1,3},{2,0},{3,1},{4,10},{5,11},{6,8},{7,9},{8,6},{9,7},{10,... | collective-permute-start | bytes 1585160 | tf_op jit(solution)/shard_map/ppermute | solution.py:492
  6.6 37.1 %collective-permute-start.1 = (f32[1032,128]{1,0:T(8,128)S(1)}, f32[1032,128]{1,0:T(8,128)S(1)}, u32[]{:S(2)}, u32[]{:S(2)}) collective-permute-start(f32[1032,128]{1,0:T(8,128)S(1)} %get-tuple-element.38), channel_id=1, source_target_pairs={{0,6},{1,7},{2,4},{3,5},{4,2},{5,3},{6,0},{7,1},{8,14},{9,15},{10,... | collective-permute-start | bytes 1585160 | tf_op jit(solution)/shard_map/ppermute | solution.py:492
  12.1 34.0 %collective-permute-start.2 = (f32[1032,128]{1,0:T(8,128)S(1)}, f32[1032,128]{1,0:T(8,128)S(1)}, u32[]{:S(2)}, u32[]{:S(2)}) collective-permute-start(f32[1032,128]{1,0:T(8,128)S(1)} %get-tuple-element.44), channel_id=1, source_target_pairs={{0,1},{1,2},{2,3},{3,0},{4,9},{5,10},{6,11},{7,8},{8,5},{9,6},{10,... | collective-permute-start | bytes 1585160 | tf_op jit(solution)/shard_map/ppermute | solution.py:492
  12.6 42.3 %collective-permute-start.3 = (f32[1032,128]{1,0:T(8,128)S(1)}, f32[1032,128]{1,0:T(8,128)S(1)}, u32[]{:S(2)}, u32[]{:S(2)}) collective-permute-start(f32[1032,128]{1,0:T(8,128)S(1)} %get-tuple-element.45), channel_id=1, source_target_pairs={{0,5},{1,6},{2,7},{3,4},{4,1},{5,2},{6,3},{7,0},{8,13},{9,14},{10,... | collective-permute-start | bytes 1585160 | tf_op jit(solution)/shard_map/ppermute | solution.py:492
  19.2 28.2 %copy-start = (f32[1,8,128,128]{3,2,1,0:T(8,128)S(1)}, f32[1,8,128,128]{3,2,1,0:T(8,128)}, u32[]{:S(2)}) copy-start(f32[1,8,128,128]{3,2,1,0:T(8,128)} %psi_ref.9) | copy-start | bytes 1572868
  19.2 28.2 %copy-start.1 = (s32[1,2,8]{2,1,0:T(2,128)S(1)}, s32[1,2,8]{2,1,0:T(2,128)}, u32[]{:S(2)}) copy-start(s32[1,2,8]{2,1,0:T(2,128)} %sizes_ref.9) | copy-start | bytes 196
  19.2 37.6 %collective-permute-start.4 = (f32[1032,128]{1,0:T(8,128)S(1)}, f32[1032,128]{1,0:T(8,128)S(1)}, u32[]{:S(2)}, u32[]{:S(2)}) collective-permute-start(f32[1032,128]{1,0:T(8,128)S(1)} %get-tuple-element.51), channel_id=1, source_target_pairs={{0,3},{1,0},{2,1},{3,2},{4,11},{5,8},{6,9},{7,10},{8,7},{9,4},{10,... | collective-permute-start | bytes 1585160 | tf_op jit(solution)/shard_map/ppermute | solution.py:492
  23.7 33.2 %collective-permute-start.5 = (f32[1032,128]{1,0:T(8,128)S(1)}, f32[1032,128]{1,0:T(8,128)S(1)}, u32[]{:S(2)}, u32[]{:S(2)}) collective-permute-start(f32[1032,128]{1,0:T(8,128)S(1)} %get-tuple-element.52), channel_id=1, source_target_pairs={{0,7},{1,4},{2,5},{3,6},{4,3},{5,0},{6,1},{7,2},{8,15},{9,12},{10,... | collective-permute-start | bytes 1585160 | tf_op jit(solution)/shard_map/ppermute | solution.py:492
  43.7 15.2 %collective-permute-start.6 = (f32[1032,128]{1,0:T(8,128)S(1)}, f32[1032,128]{1,0:T(8,128)S(1)}, u32[]{:S(2)}, u32[]{:S(2)}) collective-permute-start(f32[1032,128]{1,0:T(8,128)S(1)} %get-tuple-element.58), channel_id=1, source_target_pairs={{0,0},{1,1},{2,2},{3,3},{4,8},{5,9},{6,10},{7,11},{8,4},{9,5},{10,... | collective-permute-start | bytes 1585160 | tf_op jit(solution)/shard_map/ppermute | solution.py:492
  46.1 12.8 %collective-permute-start.7 = (f32[1032,128]{1,0:T(8,128)S(1)}, f32[1032,128]{1,0:T(8,128)S(1)}, u32[]{:S(2)}, u32[]{:S(2)}) collective-permute-start(f32[1032,128]{1,0:T(8,128)S(1)} %get-tuple-element.59), channel_id=1, source_target_pairs={{0,4},{1,5},{2,6},{3,7},{4,0},{5,1},{6,2},{7,3},{8,12},{9,13},{10,... | collective-permute-start | bytes 1585160 | tf_op jit(solution)/shard_map/ppermute | solution.py:492

commit v4 on v3

--- a/solution.py
+++ b/solution.py
@@ -223,31 +223,64 @@
     return jnp.where(odd, guess.T, guess) * live_mask(sizes_ref, owned)
 
 
-def arrive_kernel(sizes_ref, psi_ref, before_ref, alpha_ref, beta_ref, left_ref, right_ref, image_ref):
+def open_blocks(sizes_ref, psi_ref, message_ref, blocks_ref, mids_ref):
     pairs = LOCAL_TERMS // 2
     for owned in range(OWNED):
         vector = doubled(start_vector(sizes_ref, psi_ref, owned))
-        which = [owned * pairs + i for i in range(pairs)]
-        rows = slice(owned * LOCAL_TERMS * B, (owned + 1) * LOCAL_TERMS * B)
-        lefts = unpack(alpha_ref, which)
-        left_ref[rows, :] = jnp.concatenate(lefts, 0)
-        mids = [between(dot(jnp.concatenate(lefts[2 * i : 2 * i + 2], 0), vector)) for i in range(pairs)]
-        rights = jnp.concatenate(unpack(beta_ref, which), 0)
-        right_ref[rows, :] = rights
-        image_ref[owned] = before_ref[owned] + quarters(dot(jnp.concatenate(mids, 1), rights))
-
-
-def arrive(sizes, psi, before, alpha, beta):
-    block = jax.ShapeDtypeStruct((BLOCK_ROWS, 2 * B), BF16)
+        blocks = unpack(message_ref, [owned * pairs + i for i in range(pairs)])
+        for i in range(pairs):
+            both = jnp.concatenate(blocks[2 * i : 2 * i + 2], 0)
+            start = (owned * pairs + i) * 2 * B
+            blocks_ref[start : start + 2 * B, :] = both
+            mids_ref[owned, :, 2 * i * B : 2 * (i + 1) * B] = between(dot(both, vector))
+
+
+def apply_blocks(mids_ref, message_ref, blocks_ref):
+    pairs = LOCAL_TERMS // 2
+    out = []
+    for owned in range(OWNED):
+        blocks = jnp.concatenate(unpack(message_ref, [owned * pairs + i for i in range(pairs)]), 0)
+        start = owned * LOCAL_TERMS * B
+        blocks_ref[start : start + LOCAL_TERMS * B, :] = blocks
+        out.append(quarters(dot(mids_ref[owned], blocks)))
+    return jnp.stack(out, 0)
+
+
+def begin_kernel(sizes_ref, psi_ref, alpha_ref, beta_ref, next_ref, left_ref, right_ref, next_left_ref, mids_ref, image_ref, own_ref):
+    open_blocks(sizes_ref, psi_ref, alpha_ref, left_ref, own_ref)
+    image_ref[...] = apply_blocks(own_ref, beta_ref, right_ref)
+    open_blocks(sizes_ref, psi_ref, next_ref, next_left_ref, mids_ref)
+
+
+def open_kernel(sizes_ref, psi_ref, _, one_ref, two_ref, left_one_ref, left_two_ref, mids_one_ref, mids_two_ref):
+    open_blocks(sizes_ref, psi_ref, one_ref, left_one_ref, mids_one_ref)
+    open_blocks(sizes_ref, psi_ref, two_ref, left_two_ref, mids_two_ref)
+
+
+def close_kernel(*refs):
+    before_ref, mids, messages, rights, image_ref = refs[0], refs[1:4], refs[4:7], refs[7:10], refs[10]
+    image = before_ref[...]
+    for i in range(3):
+        image = image + apply_blocks(mids[i], messages[i], rights[i])
+    image_ref[...] = image
+
+
+BLOCKS = jax.ShapeDtypeStruct((BLOCK_ROWS, 2 * B), BF16)
+MIDS = jax.ShapeDtypeStruct((OWNED, 2 * B, LOCAL_TERMS * B), BF16)
+IMAGE = jax.ShapeDtypeStruct((OWNED, B, B), F32)
+
+
+def call(kernel, out_shape, name, *operands, scalars=0, scratch=()):
     return pl.pallas_call(
-        arrive_kernel,
-        out_shape=(block, block, jax.ShapeDtypeStruct((OWNED, B, B), F32)),
-        in_specs=[SMEM] + [VMEM] * 4,
-        out_specs=(VMEM,) * 3,
+        kernel,
+        out_shape=out_shape,
+        in_specs=[SMEM] * scalars + [VMEM] * (len(operands) - scalars),
+        out_specs=(VMEM,) * len(out_shape),
+        scratch_shapes=scratch,
         compiler_params=pltpu.CompilerParams(vmem_limit_bytes=16 << 20),
         cost_estimate=TINY,
-        name="arrive",
-    )(sizes, psi, before, alpha, beta)
+        name=name,
+    )(*operands)
 
 
 def krylov_kernel(sizes_ref, psi_ref, *refs):
@@ -347,10 +380,11 @@
     )(sizes, psi, *lefts, *rights, image)
 
 
-def davidson_kernel(volume, report_ref, basis_ref, out_ref, energy_ref):
+def davidson_kernel(volume, *refs):
+    *reports, basis_ref, out_ref, energy_ref = refs
     odd = lax.rem(lax.axis_index("chain"), 2) == 1
     group = lax.axis_index("term")
-    report = report_ref[...]
+    report = functools.reduce(jnp.add, [ref[...] for ref in reports])
     row_8, lane_8 = iotas(8)
 
     def column(slot):
@@ -434,26 +468,27 @@
     energy_ref[0] = energy[0, 0]
 
 
-def davidson(report, basis, volume):
+def davidson(reports, basis, volume):
     return pl.pallas_call(
         functools.partial(davidson_kernel, volume),
         out_shape=(
             jax.ShapeDtypeStruct((1, OWNED, B, B), F32),
             jax.ShapeDtypeStruct((1,), F32),
         ),
-        in_specs=[VMEM, VMEM],
+        in_specs=[VMEM] * (len(reports) + 1),
         out_specs=(VMEM, SMEM),
         compiler_params=pltpu.CompilerParams(vmem_limit_bytes=16 << 20),
         cost_estimate=TINY,
         name="davidson",
-    )(report, basis)
+    )(*reports, basis)
 
 
 ORDER = (
-    (((0, 2), (1, 2)), 20),
-    (((0, 1), (1, 1)), 20),
-    (((0, 3), (1, 3)), 20),
-    (((0, 0), (1, 0)), 20),
+    (((1, 2),), 20),
+    (((0, 2), (0, 1)), 20),
+    (((1, 1), (0, 3)), 20),
+    (((1, 3), (0, 0)), 20),
+    (((1, 0),), 20),
 )
 
 
@@ -492,19 +527,32 @@
         return lax.ppermute(message, ("chain", "term"), exchange_pairs(segments, groups, partners[side], offset))
 
     alphas, betas = {}, {}
-    for offset in (2, 1, 3, 0):
+    for offset in (2, 1, 3):
         alphas[offset] = send(0, offset)
         betas[offset] = send(1, offset)
-    lefts, rights = [], []
-    image = jnp.zeros((OWNED, B, B), F32)
-    for offset in (2, 1, 3, 0):
-        left, right, image = arrive(block_sizes, psi_guess, image, alphas[offset], betas[offset])
-        lefts.append(left)
-        rights.append(right)
+    alphas[0] = send(0, 0, betas[2])
+    betas[0] = send(1, 0, alphas[1])
+    lefts, rights = {}, {}
+    lefts[2], rights[2], lefts[1], mids_1, image = call(
+        begin_kernel, (BLOCKS, BLOCKS, BLOCKS, MIDS, IMAGE), "begin",
+        block_sizes, psi_guess, alphas[2], betas[2], alphas[1],
+        scalars=1, scratch=[pltpu.VMEM(MIDS.shape, BF16)],
+    )
+    lefts[3], lefts[0], mids_3, mids_0 = call(
+        open_kernel, (BLOCKS, BLOCKS, MIDS, MIDS), "open", block_sizes, psi_guess, image, alphas[3], alphas[0], scalars=1
+    )
+    rights[1], rights[3], rights[0], image = call(
+        close_kernel, (BLOCKS, BLOCKS, BLOCKS, IMAGE), "close",
+        image, mids_1, mids_3, mids_0, betas[1], betas[3], betas[0],
+    )
+    lefts, rights = [[side[offset] for offset in range(groups)] for side in (lefts, rights)]
     volume = float(psi_guess.shape[1] * B * B)
     basis, report = krylov(block_sizes, psi_guess, lefts, rights, image)
-    report = lax.psum(report, "term")
-    vector, energy = davidson(report, basis, volume)
+    reports = [report]
+    for shift in range(1, groups):
+        turn = [(term, (term + shift) % groups) for term in range(groups)]
+        reports.append(lax.ppermute(report, "term", turn))
+    vector, energy = davidson(reports, basis, volume)
     return vector, energy
 
 

time: 84.8 us -> 82.3 us (0.971)
  blocking collectives: 9.57 us -> 0 us
  waiting for transfers between devices: 23.3 us -> 28.4 us
  starting transfers between devices: 14.5 us -> 17.8 us
  Pallas kernels: 35.4 us -> 33.8 us
    psum x1 -> x0, blocking collectives: 9.57 us -> none  [local(): report = lax.psum(report, 'term')]
    ppermute x0 -> x3, starting transfers between devices: none -> 4.93 us  [local(): reports.append(lax.ppermute(report, 'term', turn))]
    ppermute x0 -> x3, waiting for transfers between devices: none -> 4.81 us  [local(): reports.append(lax.ppermute(report, 'term', turn))]
    ppermute x8, starting transfers between devices: 14.5 us -> 12.9 us  [send(): lax.ppermute(message, ('chain', 'term'), exchange_pairs(segments, groups,...]
    pallas_call x4 -> x3, Pallas kernels: 7.92 us -> 6.25 us  [call(): pl.pallas_call(kernel, out_shape=out_shape, in_specs=[SMEM] * scalars + [...]
    pallas_call x4 -> x5, Pallas kernels: 14.3 us -> 14.3 us  [dress(): pl.pallas_call(functools.partial(dress_kernel, segments, groups, jobs), o...]
  transfers between devices with their start and end apart: 8 -> 11, of which waited for: 2 -> 5; matrix products, arithmetic and copies ran while one was open for 0% -> 0% of each run, Pallas kernels for 20% -> 20%
where the time goes in v4:
time: 82.3 us; the launch traced here: 80.9 us
  Pallas kernels  33.8 us (41%)
  waiting for transfers between devices  28.4 us (35%)
  starting transfers between devices  17.8 us (22%)
  between operations  0.92 us (1%)
    ppermute x8, waiting for transfers between devices, send(): lax.ppermute(message, ('chain', 'term'), exchange_pairs(segments, groups,...  23.5 us
    pallas_call x5, Pallas kernels, dress(): pl.pallas_call(functools.partial(dress_kernel, segments, groups, jobs), o...  14.3 us
    ppermute x8, starting transfers between devices, send(): lax.ppermute(message, ('chain', 'term'), exchange_pairs(segments, groups,...  12.9 us
    pallas_call x1, Pallas kernels, krylov(): pl.pallas_call(krylov_kernel, out_shape=(jax.ShapeDtypeStruct((NVEC, OWNE...  12 us
    pallas_call x3, Pallas kernels, call(): pl.pallas_call(kernel, out_shape=out_shape, in_specs=[SMEM] * scalars + [...  6.25 us
    ppermute x3, starting transfers between devices, local(): reports.append(lax.ppermute(report, 'term', turn))  4.93 us
    ppermute x3, waiting for transfers between devices, local(): reports.append(lax.ppermute(report, 'term', turn))  4.81 us
  transfers between devices with their start and end apart: 11, of which 5 were waited for; matrix products, arithmetic and copies ran while one was open for 0% of the time, Pallas kernels for 20%

profile of v4, /device:TPU:2, one launch (start us, length us, event | category | flops | bytes accessed | tf_op | source)
XLA Modules:
  0.0 80.9 jit_solution(7469799078729133362)
XLA Ops:
  0.6 2.2 %dress.5 = f32[1032,128]{1,0:T(8,128)S(1)} custom-call(f32[1,8,8,128,128]{4,3,2,1,0:T(8,128)} %left_hbm.9, f32[1,8,8,128,128]{4,3,2,1,0:T(8,128)} %right_hbm.9, f32[1,8,128,128]{3,2,1,0:T(8,128)} %raw_hbm.5), custom_call_target="tpu_custom_call" | custom-call | flops 1000 | bytes 1000 | tf_op jit(solution)/shard_map/dress/pallas_call | solution.py:149
  2.9 2.6 %collective-permute-start.1 = (f32[1032,128]{1,0:T(8,128)S(1)}, f32[1032,128]{1,0:T(8,128)S(1)}, u32[]{:S(2)}, u32[]{:S(2)}) collective-permute-start(f32[1032,128]{1,0:T(8,128)S(1)} %dress.5), channel_id=1, source_target_pairs={{0,6},{1,7},{2,4},{3,5},{4,2},{5,3},{6,0},{7,1},{8,14},{9,15},{10,... | collective-permute-start | bytes 1585160 | tf_op jit(solution)/shard_map/ppermute | solution.py:527
  5.5 3.3 %dress.6 = (f32[1032,128]{1,0:T(8,128)S(1)}, f32[1032,128]{1,0:T(8,128)S(1)}) custom-call(f32[1,8,8,128,128]{4,3,2,1,0:T(8,128)} %left_hbm.9, f32[1,8,8,128,128]{4,3,2,1,0:T(8,128)} %right_hbm.9, f32[1,8,128,128]{3,2,1,0:T(8,128)} %raw_hbm.5), custom_call_target="tpu_custom_call" | custom-call | flops 1000 | bytes 1000 | tf_op jit(solution)/shard_map/dress/pallas_call | solution.py:149
  8.8 1.4 %collective-permute-start.2 = (f32[1032,128]{1,0:T(8,128)S(1)}, f32[1032,128]{1,0:T(8,128)S(1)}, u32[]{:S(2)}, u32[]{:S(2)}) collective-permute-start(f32[1032,128]{1,0:T(8,128)S(1)} %get-tuple-element.42), channel_id=1, source_target_pairs={{0,1},{1,2},{2,3},{3,0},{4,9},{5,10},{6,11},{7,8},{8,5},{9,6},{10,... | collective-permute-start | bytes 1585160 | tf_op jit(solution)/shard_map/ppermute | solution.py:527
  10.2 1.8 %collective-permute-start = (f32[1032,128]{1,0:T(8,128)S(1)}, f32[1032,128]{1,0:T(8,128)S(1)}, u32[]{:S(2)}, u32[]{:S(2)}) collective-permute-start(f32[1032,128]{1,0:T(8,128)S(1)} %get-tuple-element.40), channel_id=1, source_target_pairs={{0,2},{1,3},{2,0},{3,1},{4,10},{5,11},{6,8},{7,9},{8,6},{9,7},{10,... | collective-permute-start | bytes 1585160 | tf_op jit(solution)/shard_map/ppermute | solution.py:527
  12.0 3.3 %dress.7 = (f32[1032,128]{1,0:T(8,128)S(1)}, f32[1032,128]{1,0:T(8,128)S(1)}) custom-call(f32[1,8,8,128,128]{4,3,2,1,0:T(8,128)} %left_hbm.9, f32[1,8,8,128,128]{4,3,2,1,0:T(8,128)} %right_hbm.9, f32[1,8,128,128]{3,2,1,0:T(8,128)} %raw_hbm.5), custom_call_target="tpu_custom_call" | custom-call | flops 1000 | bytes 1000 | tf_op jit(solution)/shard_map/dress/pallas_call | solution.py:149
  15.2 3.3 %collective-permute-start.3 = (f32[1032,128]{1,0:T(8,128)S(1)}, f32[1032,128]{1,0:T(8,128)S(1)}, u32[]{:S(2)}, u32[]{:S(2)}) collective-permute-start(f32[1032,128]{1,0:T(8,128)S(1)} %get-tuple-element.47), channel_id=1, source_target_pairs={{0,3},{1,0},{2,1},{3,2},{4,11},{5,8},{6,9},{7,10},{8,7},{9,4},{10,... | collective-permute-start | bytes 1585160 | tf_op jit(solution)/shard_map/ppermute | solution.py:527
  18.5 3.3 %dress.8 = (f32[1032,128]{1,0:T(8,128)S(1)}, f32[1032,128]{1,0:T(8,128)S(1)}) custom-call(f32[1,8,8,128,128]{4,3,2,1,0:T(8,128)} %left_hbm.9, f32[1,8,8,128,128]{4,3,2,1,0:T(8,128)} %right_hbm.9, f32[1,8,128,128]{3,2,1,0:T(8,128)} %raw_hbm.5), custom_call_target="tpu_custom_call" | custom-call | flops 1000 | bytes 1000 | tf_op jit(solution)/shard_map/dress/pallas_call | solution.py:149
  21.8 0.0 copy-start
  21.8 2.3 %dress.9 = f32[1032,128]{1,0:T(8,128)S(1)} custom-call(f32[1,8,8,128,128]{4,3,2,1,0:T(8,128)} %left_hbm.9, f32[1,8,8,128,128]{4,3,2,1,0:T(8,128)} %right_hbm.9, f32[1,8,128,128]{3,2,1,0:T(8,128)} %raw_hbm.5), custom_call_target="tpu_custom_call" | custom-call | flops 1000 | bytes 1000 | tf_op jit(solution)/shard_map/dress/pallas_call | solution.py:149
  24.1 17.8 %collective-permute-done.1.beta_ref = f32[1032,128]{1,0:T(8,128)S(1)} collective-permute-done((f32[1032,128]{1,0:T(8,128)S(1)}, f32[1032,128]{1,0:T(8,128)S(1)}, u32[]{:S(2)}, u32[]{:S(2)}) %collective-permute-start.1) | collective-permute-done | bytes 528416 | tf_op jit(solution)/shard_map/ppermute | solution.py:527
  41.9 1.9 %collective-permute-start.4 = (f32[1032,128]{1,0:T(8,128)S(1)}, f32[1032,128]{1,0:T(8,128)S(1)}, u32[]{:S(2)}, u32[]{:S(2)}) collective-permute-start(f32[1032,128]{1,0:T(8,128)S(1)} %get-tuple-element.52), channel_id=1, source_target_pairs={{0,0},{1,1},{2,2},{3,3},{4,8},{5,9},{6,10},{7,11},{8,4},{9,5},{10,... | collective-permute-start | bytes 1585160 | tf_op jit(solution)/shard_map/ppermute | solution.py:527
  43.8 1.9 %collective-permute-start.7 = (f32[1032,128]{1,0:T(8,128)S(1)}, f32[1032,128]{1,0:T(8,128)S(1)}, u32[]{:S(2)}, u32[]{:S(2)}) collective-permute-start(f32[1032,128]{1,0:T(8,128)S(1)} %dress.9), channel_id=1, source_target_pairs={{0,4},{1,5},{2,6},{3,7},{4,0},{5,1},{6,2},{7,3},{8,12},{9,13},{10,... | collective-permute-start | bytes 1585160 | tf_op jit(solution)/shard_map/ppermute | solution.py:527
  45.7 2.4 %begin.1 = (bf16[2048,256]{1,0:T(8,128)(2,1)S(1)}, bf16[2048,256]{1,0:T(8,128)(2,1)S(1)}, bf16[2048,256]{1,0:T(8,128)(2,1)S(1)}, bf16[2,256,1024]{2,1,0:T(8,128)(2,1)S(1)}, f32[2,128,128]{2,1,0:T(8,128)S(1)}) custom-call(s32[1,2,8]{2,1,0:T(2,128)S(1)} %copy-done.1, f32[1,8,128,128]{3,2,1,0:T(8,128)S(1)} %copy-done, ...), custom_call_target="tpu_custom_call" | custom-call | flops 1000 | bytes 1000 | tf_op jit(solution)/shard_map/begin/pallas_call | solution.py:274
  48.1 4.3 %collective-permute-done.4.two_ref = f32[1032,128]{1,0:T(8,128)S(1)} collective-permute-done((f32[1032,128]{1,0:T(8,128)S(1)}, f32[1032,128]{1,0:T(8,128)S(1)}, u32[]{:S(2)}, u32[]{:S(2)}) %collective-permute-start.4) | collective-permute-done | bytes 528416 | tf_op jit(solution)/shard_map/ppermute | solution.py:527
  52.4 2.0 %open.1 = (bf16[2048,256]{1,0:T(8,128)(2,1)S(1)}, bf16[2048,256]{1,0:T(8,128)(2,1)S(1)}, bf16[2,256,1024]{2,1,0:T(8,128)(2,1)S(1)}, bf16[2,256,1024]{2,1,0:T(8,128)(2,1)S(1)}) custom-call(s32[1,2,8]{2,1,0:T(2,128)S(1)} %copy-done.1, f32[1,8,128,128]{3,2,1,0:T(8,128)S(1)} %copy-done, f32[2,128,128]{2,1,0:T(8,128)S(1)} %get-tuple-element.43._.refs_0_, ...), custom_call_target="tpu_custom_call" | custom-call | flops 1000 | bytes 1000 | tf_op jit(solution)/shard_map/open/pallas_call | solution.py:274
  54.5 1.4 %collective-permute-done.6.refs_5_ = f32[1032,128]{1,0:T(8,128)S(1)} collective-permute-done((f32[1032,128]{1,0:T(8,128)S(1)}, f32[1032,128]{1,0:T(8,128)S(1)}, u32[]{:S(2)}, u32[]{:S(2)}) %collective-permute-start.6) | collective-permute-done | bytes 528416 | tf_op jit(solution)/shard_map/ppermute | solution.py:527
  55.9 1.8 %close.1 = (bf16[2048,256]{1,0:T(8,128)(2,1)S(1)}, bf16[2048,256]{1,0:T(8,128)(2,1)S(1)}, bf16[2048,256]{1,0:T(8,128)(2,1)S(1)}, f32[2,128,128]{2,1,0:T(8,128)S(1)}) custom-call(f32[2,128,128]{2,1,0:T(8,128)S(1)} %get-tuple-element.43._.refs_0_, bf16[2,256,1024]{2,1,0:T(8,128)(2,1)S(1)} %get-tuple-element.57.refs_1_, ...), custom_call_target="tpu_custom_call" | custom-call | flops 1000 | bytes 1000 | tf_op jit(solution)/shard_map/close/pallas_call | solution.py:274
  57.7 12.0 %krylov.1 = (f32[6,2,128,128]{3,2,1,0:T(8,128)S(1)}, f32[8,128]{1,0:T(8,128)S(1)}) custom-call(s32[1,2,8]{2,1,0:T(2,128)S(1)} %copy-done.1, f32[1,8,128,128]{3,2,1,0:T(8,128)S(1)} %copy-done, bf16[2048,256]{1,0:T(8,128)(2,1)S(1)} %get-tuple-element.53.refs_0_, bf16[2048,256]{1,0:T(8,128)(2,1)S(1)} %get-tuple-element.54.refs_1_, ...), custom_call_target="tpu_custom_call" | custom-call | flops 1000 | bytes 1000 | tf_op jit(solution)/shard_map/krylov/pallas_call | solution.py:364
  69.7 3.1 %collective-permute-start.10 = (f32[8,128]{1,0:T(8,128)S(1)}, f32[8,128]{1,0:T(8,128)S(1)}, u32[]{:S(2)}, u32[]{:S(2)}) collective-permute-start(f32[8,128]{1,0:T(8,128)S(1)} %get-tuple-element.70.refs_0_), channel_id=1, source_target_pairs={{0,3},{1,0},{2,1},{3,2},{4,7},{5,4},{6,5},{7,6},{8,11},{9,8},{10,9... | collective-permute-start | bytes 12296 | tf_op jit(solution)/shard_map/ppermute | solution.py:554
  72.9 1.8 %collective-permute-start.9 = (f32[8,128]{1,0:T(8,128)S(1)}, f32[8,128]{1,0:T(8,128)S(1)}, u32[]{:S(2)}, u32[]{:S(2)}) collective-permute-start(f32[8,128]{1,0:T(8,128)S(1)} %get-tuple-element.70.refs_0_), channel_id=1, source_target_pairs={{0,2},{1,3},{2,0},{3,1},{4,6},{5,7},{6,4},{7,5},{8,10},{9,11},{10,... | collective-permute-start | bytes 12296 | tf_op jit(solution)/shard_map/ppermute | solution.py:554
  74.7 3.3 %collective-permute-done.9.refs_2_ = f32[8,128]{1,0:T(8,128)S(1)} collective-permute-done((f32[8,128]{1,0:T(8,128)S(1)}, f32[8,128]{1,0:T(8,128)S(1)}, u32[]{:S(2)}, u32[]{:S(2)}) %collective-permute-start.9) | collective-permute-done | bytes 4128 | tf_op jit(solution)/shard_map/ppermute | solution.py:554
  78.0 1.5 %collective-permute-done.8.refs_1_ = f32[8,128]{1,0:T(8,128)S(1)} collective-permute-done((f32[8,128]{1,0:T(8,128)S(1)}, f32[8,128]{1,0:T(8,128)S(1)}, u32[]{:S(2)}, u32[]{:S(2)}) %collective-permute-start.8) | collective-permute-done | bytes 4128 | tf_op jit(solution)/shard_map/ppermute | solution.py:554
  79.5 1.2 %davidson.1 = (f32[1,2,128,128]{3,2,1,0:T(8,128)}, f32[1]{0:T(128)}) custom-call(f32[8,128]{1,0:T(8,128)S(1)} %get-tuple-element.70.refs_0_, f32[8,128]{1,0:T(8,128)S(1)} %collective-permute-done.8.refs_1_, f32[8,128]{1,0:T(8,128)S(1)} %collective-permute-done.9.refs_2_, f32[8,128]{1,0:T(8,128)S(1)} %collective-permute-done.10.refs_3_, ...), custom_call_target="tpu_custom_call" | custom-call | flops 1000 | bytes 1000 | tf_op jit(solution)/shard_map/davidson/pallas_call | solution.py:472
  (12 shorter events, 0.0 us)
Async XLA Ops:
  2.9 39.0 %collective-permute-start.1 = (f32[1032,128]{1,0:T(8,128)S(1)}, f32[1032,128]{1,0:T(8,128)S(1)}, u32[]{:S(2)}, u32[]{:S(2)}) collective-permute-start(f32[1032,128]{1,0:T(8,128)S(1)} %dress.5), channel_id=1, source_target_pairs={{0,6},{1,7},{2,4},{3,5},{4,2},{5,3},{6,0},{7,1},{8,14},{9,15},{10,... | collective-permute-start | bytes 1585160 | tf_op jit(solution)/shard_map/ppermute | solution.py:527
  8.8 33.1 %collective-permute-start.2 = (f32[1032,128]{1,0:T(8,128)S(1)}, f32[1032,128]{1,0:T(8,128)S(1)}, u32[]{:S(2)}, u32[]{:S(2)}) collective-permute-start(f32[1032,128]{1,0:T(8,128)S(1)} %get-tuple-element.42), channel_id=1, source_target_pairs={{0,1},{1,2},{2,3},{3,0},{4,9},{5,10},{6,11},{7,8},{8,5},{9,6},{10,... | collective-permute-start | bytes 1585160 | tf_op jit(solution)/shard_map/ppermute | solution.py:527
  10.2 33.6 %collective-permute-start = (f32[1032,128]{1,0:T(8,128)S(1)}, f32[1032,128]{1,0:T(8,128)S(1)}, u32[]{:S(2)}, u32[]{:S(2)}) collective-permute-start(f32[1032,128]{1,0:T(8,128)S(1)} %get-tuple-element.40), channel_id=1, source_target_pairs={{0,2},{1,3},{2,0},{3,1},{4,10},{5,11},{6,8},{7,9},{8,6},{9,7},{10,... | collective-permute-start | bytes 1585160 | tf_op jit(solution)/shard_map/ppermute | solution.py:527
  15.2 32.9 %collective-permute-start.3 = (f32[1032,128]{1,0:T(8,128)S(1)}, f32[1032,128]{1,0:T(8,128)S(1)}, u32[]{:S(2)}, u32[]{:S(2)}) collective-permute-start(f32[1032,128]{1,0:T(8,128)S(1)} %get-tuple-element.47), channel_id=1, source_target_pairs={{0,3},{1,0},{2,1},{3,2},{4,11},{5,8},{6,9},{7,10},{8,7},{9,4},{10,... | collective-permute-start | bytes 1585160 | tf_op jit(solution)/shard_map/ppermute | solution.py:527
  18.5 36.0 %collective-permute-start.5 = (f32[1032,128]{1,0:T(8,128)S(1)}, f32[1032,128]{1,0:T(8,128)S(1)}, u32[]{:S(2)}, u32[]{:S(2)}) collective-permute-start(f32[1032,128]{1,0:T(8,128)S(1)} %get-tuple-element.60), channel_id=1, source_target_pairs={{0,5},{1,6},{2,7},{3,4},{4,1},{5,2},{6,3},{7,0},{8,13},{9,14},{10,... | collective-permute-start | bytes 1585160 | tf_op jit(solution)/shard_map/ppermute | solution.py:527
  21.8 23.9 %copy-start = (f32[1,8,128,128]{3,2,1,0:T(8,128)S(1)}, f32[1,8,128,128]{3,2,1,0:T(8,128)}, u32[]{:S(2)}) copy-start(f32[1,8,128,128]{3,2,1,0:T(8,128)} %psi_ref.5) | copy-start | bytes 1572868
  21.8 23.9 %copy-start.1 = (s32[1,2,8]{2,1,0:T(2,128)S(1)}, s32[1,2,8]{2,1,0:T(2,128)}, u32[]{:S(2)}) copy-start(s32[1,2,8]{2,1,0:T(2,128)} %sizes_ref.5) | copy-start | bytes 196
  41.9 14.0 %collective-permute-start.6 = (f32[1032,128]{1,0:T(8,128)S(1)}, f32[1032,128]{1,0:T(8,128)S(1)}, u32[]{:S(2)}, u32[]{:S(2)}) collective-permute-start(f32[1032,128]{1,0:T(8,128)S(1)} %get-tuple-element.61), channel_id=1, source_target_pairs={{0,7},{1,4},{2,5},{3,6},{4,3},{5,0},{6,1},{7,2},{8,15},{9,12},{10,... | collective-permute-start | bytes 1585160 | tf_op jit(solution)/shard_map/ppermute | solution.py:527
  41.9 10.5 %collective-permute-start.4 = (f32[1032,128]{1,0:T(8,128)S(1)}, f32[1032,128]{1,0:T(8,128)S(1)}, u32[]{:S(2)}, u32[]{:S(2)}) collective-permute-start(f32[1032,128]{1,0:T(8,128)S(1)} %get-tuple-element.52), channel_id=1, source_target_pairs={{0,0},{1,1},{2,2},{3,3},{4,8},{5,9},{6,10},{7,11},{8,4},{9,5},{10,... | collective-permute-start | bytes 1585160 | tf_op jit(solution)/shard_map/ppermute | solution.py:527
  43.8 12.1 %collective-permute-start.7 = (f32[1032,128]{1,0:T(8,128)S(1)}, f32[1032,128]{1,0:T(8,128)S(1)}, u32[]{:S(2)}, u32[]{:S(2)}) collective-permute-start(f32[1032,128]{1,0:T(8,128)S(1)} %dress.9), channel_id=1, source_target_pairs={{0,4},{1,5},{2,6},{3,7},{4,0},{5,1},{6,2},{7,3},{8,12},{9,13},{10,... | collective-permute-start | bytes 1585160 | tf_op jit(solution)/shard_map/ppermute | solution.py:527
  69.7 4.9 %collective-permute-start.10 = (f32[8,128]{1,0:T(8,128)S(1)}, f32[8,128]{1,0:T(8,128)S(1)}, u32[]{:S(2)}, u32[]{:S(2)}) collective-permute-start(f32[8,128]{1,0:T(8,128)S(1)} %get-tuple-element.70.refs_0_), channel_id=1, source_target_pairs={{0,3},{1,0},{2,1},{3,2},{4,7},{5,4},{6,5},{7,6},{8,11},{9,8},{10,9... | collective-permute-start | bytes 12296 | tf_op jit(solution)/shard_map/ppermute | solution.py:554
  72.9 5.1 %collective-permute-start.9 = (f32[8,128]{1,0:T(8,128)S(1)}, f32[8,128]{1,0:T(8,128)S(1)}, u32[]{:S(2)}, u32[]{:S(2)}) collective-permute-start(f32[8,128]{1,0:T(8,128)S(1)} %get-tuple-element.70.refs_0_), channel_id=1, source_target_pairs={{0,2},{1,3},{2,0},{3,1},{4,6},{5,7},{6,4},{7,5},{8,10},{9,11},{10,... | collective-permute-start | bytes 12296 | tf_op jit(solution)/shard_map/ppermute | solution.py:554
  74.7 4.8 %collective-permute-start.8 = (f32[8,128]{1,0:T(8,128)S(1)}, f32[8,128]{1,0:T(8,128)S(1)}, u32[]{:S(2)}, u32[]{:S(2)}) collective-permute-start(f32[8,128]{1,0:T(8,128)S(1)} %get-tuple-element.70.refs_0_), channel_id=1, source_target_pairs={{0,1},{1,2},{2,3},{3,0},{4,5},{5,6},{6,7},{7,4},{8,9},{9,10},{10,1... | collective-permute-start | bytes 12296 | tf_op jit(solution)/shard_map/ppermute | solution.py:554
